TPU v7x, 128 devices: a whole 4x4x4 slice. The times are simulated.
128 devices in a mesh: gx: 8 (over z, core), yz: 16 (over y, x).
Axes of the slice: x: 4, y: 4, z: 4, core: 2. Of those that a mesh axis runs over, the one named last changes fastest.
Arguments:
- field: float32 [144, 262144], P(None, ('gx', 'yz')), may hold values from -6 to 6
- edge_signs: int32 [12, 262144], P(None, ('gx', 'yz')), may hold values from -1 to 1, as said below
- face_nbrs: int32 [6, 262144], P(None, ('gx', 'yz')), may hold values from -1 to 262143, as said below
- elem_size: float32 [262144], P(('gx', 'yz')), may hold values from 0.5 to 2
- mu_inv: float32 [262144], P(('gx', 'yz')), may hold values from 0.25 to 4
- permittivity: float32 [262144], P(('gx', 'yz')), may hold values from 0.25 to 4
- new_owner: int32 [262144, 1], P(('gx', 'yz')), may hold values from 0 to 127; in each aligned block of 2048 rows (0 to 2047, 2048 to 4095, ...) at most 32 rows name the same one
- trace_map: float32 [144, 144], replicated, may hold values from -0.5 to 0.5
- stiffness: float32 [144, 144], replicated, may hold values from -0.5 to 0.5
- mass: float32 [144, 144], replicated, may hold values from -0.5 to 0.5
Outputs:
- indicators: float32 [262144], P(('gx', 'yz'))
- migrated: float32 [144, 524288], P(None, ('gx', 'yz'))
- applied: float32 [144, 524288], P(None, ('gx', 'yz'))
Inputs may be any that keep to these rules, and one draw needn't show every extreme that they name: `edge_signs`: each entry is -1 or 1. `face_nbrs`: A neighbour of an element of device block b (elements b * 2048 to (b + 1) * 2048 - 1) lies in block b - 1, b or b + 1, or is -1. `new_owner`: within the elements of one device no device number appears more than 32 times, and some device receives exactly 32 from some device.
All inputs are finite; a program needn't handle non-finite values.
Results may differ from a plain program's by a relative error of at most 0.0003.
Values sent between devices are 32-bit elements; how exact they have to be, the bound alone decides.
A program may use at most 64 MiB of HBM per device.

v0:
```python
import jax
import jax.numpy as jnp
import numpy as np
from jax import lax
from jax.sharding import PartitionSpec as P


def with_halo(cells, sides, width):
    for axis, dim in sides:
        count = lax.axis_size(axis)
        ends = count - 1
        head = lax.slice_in_dim(cells, 0, width, axis=dim)
        tail = lax.slice_in_dim(cells, cells.shape[dim] - width, cells.shape[dim], axis=dim)
        cells = jnp.concatenate(
            [
                lax.ppermute(tail, axis, [(i, (i + 1) % count) for i in range(ends)]),
                cells,
                lax.ppermute(head, axis, [((i + 1) % count, i) for i in range(ends)]),
            ],
            axis=dim,
        )
    return cells


def expansion():
    table = np.zeros((12, 144), np.float32)
    for i in range(36):
        if i % 3 != 1:
            table[i // 3, i] = 1.0
    return jnp.asarray(table)


def left_product(matrix, coeffs):
    return lax.dot_general(
        matrix, coeffs, (((0,), (0,)), ((), ())), precision=lax.Precision.HIGHEST
    )


def element_apply(coeffs, mu_part, eps_part, stiffness, mass):
    return mu_part[None, :] * left_product(stiffness, coeffs) + eps_part[None, :] * left_product(
        mass, coeffs
    )


def body(
    field,
    edge_signs,
    face_nbrs,
    elem_size,
    mu_inv,
    permittivity,
    new_owner,
    trace_map,
    stiffness,
    mass,
):
    dofs, e_dev = field.shape
    face_width = trace_map.shape[1] // 6
    devices = lax.axis_size(("gx", "yz"))
    slot_cap = 2 * e_dev // devices
    total = devices * slot_cap
    shifted = (edge_signs - 1).astype(jnp.float32)
    oriented = field * (1.0 + left_product(expansion(), shifted))
    traces = left_product(trace_map, oriented)
    extended = with_halo(traces, ((("gx", "yz"), 1),), e_dev)
    me_index = lax.axis_index(("gx", "yz"))
    valid = face_nbrs >= 0
    marked = jnp.where(valid, face_nbrs - (me_index - 1) * e_dev, 0)
    squares = jnp.zeros((e_dev,), jnp.float32)
    for face in range(6):
        other = face ^ 1
        picked = jnp.take(
            extended[other * face_width : (other + 1) * face_width], marked[face], axis=1
        )
        across = jnp.where(valid[face][None, :], picked, 0.0)
        jump = traces[face * face_width : (face + 1) * face_width] - across
        squares = squares + jnp.sum(jump * jump, axis=0)
    indicators = jnp.sqrt(elem_size * (squares / (6 * face_width)) + 1e-06)
    owner = new_owner[:, 0]
    onehot = (owner[:, None] == jnp.arange(devices, dtype=jnp.int32)[None, :]).astype(jnp.int32)
    rank = jnp.sum(onehot * jnp.cumsum(onehot, axis=0), axis=1) - 1
    slot = owner * slot_cap + rank
    stacked = jnp.concatenate([oriented, mu_inv[None, :], permittivity[None, :]], axis=0)
    payload = jnp.zeros((stacked.shape[0], total), jnp.float32).at[:, slot].set(stacked)
    received = lax.all_to_all(payload, ("gx", "yz"), split_axis=1, concat_axis=1, tiled=True)
    migrated = received[:dofs]
    applied = element_apply(migrated, received[dofs], received[dofs + 1], stiffness, mass)
    return (indicators, migrated, applied)


def solution(mesh):
    in_specs = (
        P(None, ("gx", "yz")),
        P(None, ("gx", "yz")),
        P(None, ("gx", "yz")),
        P(("gx", "yz")),
        P(("gx", "yz")),
        P(("gx", "yz")),
        P(("gx", "yz"), None),
        P(),
        P(),
        P(),
    )
    out_specs = (P(("gx", "yz")), P(None, ("gx", "yz")), P(None, ("gx", "yz")))
    return jax.shard_map(body, mesh=mesh, in_specs=in_specs, out_specs=out_specs, check_vma=False)
```

profile of v0, /device:TPU:26, one launch (start us, length us, event | category | flops | bytes accessed | tf_op | source)
XLA Modules:
  0.0 152.0 jit_solution(2030901055575975140)
XLA Ops:
  0.7 2.5 %fusion.3 = f32[144,2048]{1,0:T(8,128)S(1)} fusion(f32[144,2048]{1,0:T(8,128)} %param.13, f32[12,144]{1,0:T(8,128)} %constant.54.clone, s32[12,2048]{1,0:T(8,128)} %param.14), kind=kOutput, calls=%fused_computation.14 | convolution fusion | flops 43106304 | bytes 2464512 | tf_op jit(solution)/shard_map/dot_general | solution.py:34
  3.2 1.2 convolution_bitcast_fusion
  4.5 3.4 %collective-permute-start = (f32[144,2048]{1,0:T(8,128)S(1)}, f32[144,2048]{1,0:T(8,128)}, u32[]{:S(2)}, u32[]{:S(2)}) collective-permute-start(f32[144,2048]{1,0:T(8,128)S(1)} %convolution_bitcast_fusion), channel_id=1, source_target_pairs={{0,1},{1,2},{2,3},{3,4},{4,5},{5,6},{6,7},{7,8},{8,9},{9,10},{10,1... | collective-permute-start | bytes 3538952 | tf_op jit(solution)/shard_map/ppermute | solution.py:16
  7.9 2.5 %collective-permute-start.1 = (f32[144,2048]{1,0:T(8,128)S(1)}, f32[144,2048]{1,0:T(8,128)}, u32[]{:S(2)}, u32[]{:S(2)}) collective-permute-start(f32[144,2048]{1,0:T(8,128)S(1)} %convolution_bitcast_fusion), channel_id=1, source_target_pairs={{1,0},{2,1},{3,2},{4,3},{5,4},{6,5},{7,6},{8,7},{9,8},{10,9},{11,1... | collective-permute-start | bytes 3538952 | tf_op jit(solution)/shard_map/ppermute | solution.py:18
  10.3 0.7 copy.59
  11.1 1.2 fusion.7
  12.2 0.6 slice_bitcast_fusion
  12.8 1.3 reduce-window.9
  14.2 0.7 slice.159
  15.0 0.3 copy.60
  15.3 0.6 fusion.6
  16.0 1.1 maximum_bitcast_fusion
  17.1 1.8 %copy.61 = f32[2048,146]{1,0:T(8,128)S(1)} copy(f32[2048,146]{0,1:T(8,128)} %maximum_bitcast_fusion) | data formatting | bytes 2392064 | tf_op jit(solution)/shard_map/concatenate | solution.py:83
  18.9 11.2 %scatter_custom_fusion = f32[146,4096]{0,1:T(8,128)} fusion(s32[2048]{0:T(1024)S(1)} %bitcast.82, f32[2048,146]{1,0:T(8,128)S(1)} %copy.61, f32[]{:T(128)} %constant.20.clone.1), kind=kCustom, calls=%fused_computation.18 | custom fusion | bytes 2392068 | tf_op jit(solution)/shard_map/scatter | solution.py:84
  30.2 10.7 %all-to-all-start = ((f32[146,128,32]{0,2,1:T(8,128)}), f32[146,128,32]{0,2,1:T(8,128)}, u32[]{:S(2)}, u32[]{:S(2)}) async-start(f32[146,128,32]{0,2,1:T(8,128)} %bitcast.64), calls=%async_computation | async-start | bytes 8388608 | tf_op jit(solution)/shard_map/all_to_all | solution.py:85
  41.0 0.6 fusion.26
  41.6 0.7 slice_reduce_fusion.6
  42.4 0.6 fusion.25
  43.0 0.6 fusion.27
  43.6 0.6 compare_and_fusion
  44.2 0.5 compare_and_fusion.2
  44.7 0.5 compare_and_fusion.3
  45.3 1.9 %pad_maximum_fusion = f32[144,6144]{1,0:T(8,128)S(1)} fusion(f32[144,2048]{1,0:T(8,128)} %collective-permute-done.1, f32[144,2048]{1,0:T(8,128)S(1)} %convolution_bitcast_fusion, f32[144,2048]{1,0:T(8,128)} %collective-permute-done), kind=kLoop, calls=%fused_computation.11 | loop fusion | flops 1769472 | bytes 7077888 | tf_op jit(solution)/shard_map/concatenate | solution.py:14
  47.2 1.3 fusion.32
  48.5 3.2 %copy.53 = f32[24,6144]{0,1:T(8,128)} copy(f32[24,6144]{1,0:T(8,128)} %get-tuple-element.27) | data formatting | bytes 1179648 | tf_op jit(solution)/shard_map/slice | solution.py:73
  51.6 9.5 %gather_fusion.3 = f32[2048,24]{1,0:T(8,128)} fusion(f32[24,6144]{0,1:T(8,128)} %copy.53, s32[2048]{0:T(1024)S(1)} %fusion.28), kind=kCustom, calls=%fused_computation.3.clone | custom fusion | bytes 401408 | tf_op jit(solution)/shard_map/jit(_take)/gather | solution.py:72
  61.2 2.2 %copy.54 = f32[2048,24]{0,1:T(8,128)} copy(f32[2048,24]{1,0:T(8,128)} %gather_fusion.3) | data formatting | bytes 393216 | tf_op jit(solution)/shard_map/jit(_take)/gather | solution.py:72
  63.4 3.2 %copy.55 = f32[24,6144]{0,1:T(8,128)} copy(f32[24,6144]{1,0:T(8,128)} %get-tuple-element.26) | data formatting | bytes 1179648 | tf_op jit(solution)/shard_map/slice | solution.py:73
  66.6 9.5 %gather_fusion.4 = f32[2048,24]{1,0:T(8,128)} fusion(f32[24,6144]{0,1:T(8,128)} %copy.55, s32[2048]{0:T(1024)S(1)} %fusion.29), kind=kCustom, calls=%fused_computation.4.clone | custom fusion | bytes 401408 | tf_op jit(solution)/shard_map/jit(_take)/gather | solution.py:72
  76.1 2.2 %copy.56 = f32[2048,24]{0,1:T(8,128)} copy(f32[2048,24]{1,0:T(8,128)} %gather_fusion.4) | data formatting | bytes 393216 | tf_op jit(solution)/shard_map/jit(_take)/gather | solution.py:72
  78.3 3.2 %copy.57 = f32[24,6144]{0,1:T(8,128)} copy(f32[24,6144]{1,0:T(8,128)} %get-tuple-element.25) | data formatting | bytes 1179648 | tf_op jit(solution)/shard_map/slice | solution.py:73
  81.5 9.5 %gather_fusion.5 = f32[2048,24]{1,0:T(8,128)} fusion(f32[24,6144]{0,1:T(8,128)} %copy.57, s32[2048]{0:T(1024)S(1)} %fusion.30), kind=kCustom, calls=%fused_computation.5.clone | custom fusion | bytes 401408 | tf_op jit(solution)/shard_map/jit(_take)/gather | solution.py:72
  91.0 2.2 %copy.58 = f32[2048,24]{0,1:T(8,128)} copy(f32[2048,24]{1,0:T(8,128)} %gather_fusion.5) | data formatting | bytes 393216 | tf_op jit(solution)/shard_map/jit(_take)/gather | solution.py:72
  93.2 2.3 %copy.49 = f32[24,6144]{0,1:T(8,128)} copy(f32[24,6144]{1,0:T(8,128)S(1)} %get-tuple-element.28) | data formatting | bytes 1179648 | tf_op jit(solution)/shard_map/slice | solution.py:73
  95.5 8.3 %gather_fusion.1 = f32[2048,24]{1,0:T(8,128)S(1)} fusion(f32[24,6144]{0,1:T(8,128)} %copy.49, s32[2048]{0:T(1024)} %fusion.26), kind=kCustom, calls=%fused_computation.1.clone | custom fusion | bytes 401408 | tf_op jit(solution)/shard_map/jit(_take)/gather | solution.py:72
  103.8 1.0 copy.50
  104.8 2.3 %copy.47 = f32[24,6144]{0,1:T(8,128)} copy(f32[24,6144]{1,0:T(8,128)S(1)} %get-tuple-element.29) | data formatting | bytes 1179648 | tf_op jit(solution)/shard_map/slice | solution.py:73
  107.1 7.3 %gather_fusion = f32[2048,24]{1,0:T(8,128)S(1)} fusion(f32[24,6144]{0,1:T(8,128)} %copy.47, s32[2048]{0:T(1024)S(1)} %copy-done.11), kind=kCustom, calls=%fused_computation.clone | custom fusion | bytes 401408 | tf_op jit(solution)/shard_map/jit(_take)/gather | solution.py:72
  114.5 0.3 copy.48
  114.8 2.3 %copy.51 = f32[24,6144]{0,1:T(8,128)} copy(f32[24,6144]{1,0:T(8,128)S(1)} %get-tuple-element.24) | data formatting | bytes 1179648 | tf_op jit(solution)/shard_map/slice | solution.py:73
  117.1 7.4 %gather_fusion.2 = f32[2048,24]{1,0:T(8,128)S(1)} fusion(f32[24,6144]{0,1:T(8,128)} %copy.51, s32[2048]{0:T(1024)S(1)} %copy-done.10), kind=kCustom, calls=%fused_computation.2.clone | custom fusion | bytes 401408 | tf_op jit(solution)/shard_map/jit(_take)/gather | solution.py:72
  124.8 0.8 fusion.21
  125.6 0.9 fusion.19
  126.6 0.6 add_sqrt_fusion
  127.2 4.5 %slice_reduce_fusion = (f32[128,32]{1,0:T(8,128)S(1)}, f32[128,32]{1,0:T(8,128)S(1)}) fusion(f32[146,128,32]{0,2,1:T(8,128)} %all-to-all-done), kind=kLoop, calls=%fused_computation.16 | loop fusion | bytes 65536 | tf_op jit(solution)/shard_map/slice | solution.py:87
  131.9 5.0 %copy.62 = f32[144,4096]{1,0:T(8,128)} copy(f32[144,4096]{0,1:T(8,128)} %bitcast.25) | data formatting | bytes 4718592
  136.8 6.9 %convolution_multiply_fusion.1 = f32[4096,144]{0,1:T(8,128)S(1)} fusion(f32[144,4096]{0,1:T(8,128)} %bitcast.25, f32[144,144]{1,0:T(8,128)S(1)} %copy-done, f32[4096]{0:T(1024)S(1)} %mul.75), kind=kOutput, calls=%fused_computation.9 | convolution fusion | flops 1019805696 | bytes 4817920 | tf_op jit(solution)/shard_map/dot_general | solution.py:34
  143.7 8.3 %fusion.1 = f32[144,4096]{1,0:T(8,128)} fusion(f32[4096,144]{0,1:T(8,128)S(1)} %convolution_multiply_fusion.1, f32[144,4096]{0,1:T(8,128)} %bitcast.25, f32[144,144]{1,0:T(8,128)S(1)} %copy-done.7, f32[4096]{0:T(1024)S(1)} %mul.78), kind=kOutput, calls=%fused_computation.10 | convolution fusion | flops 1020395520 | bytes 7177216 | tf_op jit(solution)/shard_map/dot_general | solution.py:34
  (45 shorter events, 0.7 us)
Async XLA Ops:
  0.6 136.2 %copy-start = (f32[144,144]{1,0:T(8,128)S(1)}, f32[144,144]{1,0:T(8,128)}, u32[]{:S(2)}) copy-start(f32[144,144]{1,0:T(8,128)} %param.21) | copy-start | bytes 248836
  0.6 2.6 %copy-start.6 = (f32[144,144]{1,0:T(8,128)S(1)}, f32[144,144]{1,0:T(8,128)}, u32[]{:S(2)}) copy-start(f32[144,144]{1,0:T(8,128)} %param.20) | copy-start | bytes 248836
  0.7 9.7 %copy-start.8 = (s32[2048,1]{0,1:T(1,128)S(1)}, s32[2048,1]{0,1:T(1,128)}, u32[]{:S(2)}) copy-start(s32[2048,1]{0,1:T(1,128)} %param.19) | copy-start | bytes 24580
  4.5 40.8 %collective-permute-start = (f32[144,2048]{1,0:T(8,128)S(1)}, f32[144,2048]{1,0:T(8,128)}, u32[]{:S(2)}, u32[]{:S(2)}) collective-permute-start(f32[144,2048]{1,0:T(8,128)S(1)} %convolution_bitcast_fusion), channel_id=1, source_target_pairs={{0,1},{1,2},{2,3},{3,4},{4,5},{5,6},{6,7},{7,8},{8,9},{9,10},{10,1... | collective-permute-start | bytes 3538952 | tf_op jit(solution)/shard_map/ppermute | solution.py:16
  7.9 37.4 %collective-permute-start.1 = (f32[144,2048]{1,0:T(8,128)S(1)}, f32[144,2048]{1,0:T(8,128)}, u32[]{:S(2)}, u32[]{:S(2)}) collective-permute-start(f32[144,2048]{1,0:T(8,128)S(1)} %convolution_bitcast_fusion), channel_id=1, source_target_pairs={{1,0},{2,1},{3,2},{4,3},{5,4},{6,5},{7,6},{8,7},{9,8},{10,9},{11,1... | collective-permute-start | bytes 3538952 | tf_op jit(solution)/shard_map/ppermute | solution.py:18
  14.2 1.1 copy-start.9
  14.9 1.1 copy-start.12
  14.9 1.1 copy-start.13
  30.2 10.7 %copy-start.5 = (s32[6,2048]{1,0:T(8,128)S(1)}, s32[6,2048]{1,0:T(8,128)}, u32[]{:S(2)}) copy-start(s32[6,2048]{1,0:T(8,128)} %param.15) | copy-start | bytes 147460
  30.2 97.1 %all-to-all-start = ((f32[146,128,32]{0,2,1:T(8,128)}), f32[146,128,32]{0,2,1:T(8,128)}, u32[]{:S(2)}, u32[]{:S(2)}) async-start(f32[146,128,32]{0,2,1:T(8,128)} %bitcast.64), calls=%async_computation | async-start | bytes 8388608 | tf_op jit(solution)/shard_map/all_to_all | solution.py:85
  104.8 2.3 %copy-start.11 = (s32[2048]{0:T(1024)S(1)}, s32[2048]{0:T(1024)}, u32[]{:S(2)}) copy-start(s32[2048]{0:T(1024)} %fusion.25) | copy-start | bytes 24580
  114.5 2.6 %copy-start.10 = (s32[2048]{0:T(1024)S(1)}, s32[2048]{0:T(1024)}, u32[]{:S(2)}) copy-start(s32[2048]{0:T(1024)} %fusion.27) | copy-start | bytes 24580
  117.1 8.5 %copy-start.1 = (f32[2048,24]{0,1:T(8,128)S(1)}, f32[2048,24]{0,1:T(8,128)}, u32[]{:S(2)}) copy-start(f32[2048,24]{0,1:T(8,128)} %copy.54) | copy-start | bytes 589828
  117.1 8.5 %copy-start.2 = (f32[2048,24]{0,1:T(8,128)S(1)}, f32[2048,24]{0,1:T(8,128)}, u32[]{:S(2)}) copy-start(f32[2048,24]{0,1:T(8,128)} %copy.56) | copy-start | bytes 589828
  117.1 8.5 %copy-start.3 = (f32[2048,24]{0,1:T(8,128)S(1)}, f32[2048,24]{0,1:T(8,128)}, u32[]{:S(2)}) copy-start(f32[2048,24]{0,1:T(8,128)} %copy.58) | copy-start | bytes 589828
  117.1 8.5 %copy-start.4 = (f32[2048,24]{0,1:T(8,128)S(1)}, f32[2048,24]{0,1:T(8,128)}, u32[]{:S(2)}) copy-start(f32[2048,24]{0,1:T(8,128)} %copy.50) | copy-start | bytes 589828
  124.8 1.8 %copy-start.14 = (f32[2048]{0:T(1024)S(1)}, f32[2048]{0:T(1024)}, u32[]{:S(2)}) copy-start(f32[2048]{0:T(1024)} %param.16) | copy-start | bytes 24580
  136.8 6.9 %copy-start.7 = (f32[144,144]{1,0:T(8,128)S(1)}, f32[144,144]{1,0:T(8,128)}, u32[]{:S(2)}) copy-start(f32[144,144]{1,0:T(8,128)} %param.22) | copy-start | bytes 248836
where the time goes:
time: 154 us; the launch traced here: 152 us
  local copies, waits for them, and re-layouts  103 us (67%)
  matrix products  18.9 us (12%)
  starting transfers between devices  16.6 us (11%)
  other arithmetic  12.1 us (8%)
    gather x12, local copies, waits for them, and re-layouts, body(): jnp.take(extended[other * face_width:(other + 1) * face_width], marked[fa...  59.8 us
    dot_general x4, matrix products, left_product(): lax.dot_general(matrix, coeffs, (((0,), (0,)), ((), ())), precision=lax.P...  18.9 us
    slice x7, local copies, waits for them, and re-layouts, body(): extended[other * face_width:(other + 1) * face_width]  17.7 us
    scatter x1, local copies, waits for them, and re-layouts, body(): jnp.zeros((stacked.shape[0], total), jnp.float32).at[:, slot].set(stacked)  11.2 us
    all_to_all x1, starting transfers between devices, body(): lax.all_to_all(payload, ('gx', 'yz'), split_axis=1, concat_axis=1, tiled=...  10.7 us
    unnamed x31, local copies, waits for them, and re-layouts  5.03 us
    slice x1, local copies, waits for them, and re-layouts, body(): received[dofs + 1]  4.48 us
    ppermute x1, starting transfers between devices, with_halo(): lax.ppermute(tail, axis, [(i, (i + 1) % count) for i in range(ends)])  3.39 us
  transfers between devices with their start and end apart: 3, of which 0 were waited for; matrix products, arithmetic and copies ran while one was open for 70% of the time, Pallas kernels for 0%

commit v1 on v0

v1 whole, which is shorter than its diff:
```python
import functools

import jax
import jax.numpy as jnp
from jax import lax
from jax.experimental import pallas as pl
from jax.experimental.pallas import tpu as pltpu
from jax.sharding import PartitionSpec as P

AXES = ("gx", "yz")
LANES = 128
VMEM_LIMIT = 40 << 20


def split3(value):
    high = value.astype(jnp.bfloat16)
    low = (value - high.astype(jnp.float32)).astype(jnp.bfloat16)
    return high, low


def product3(left, right):
    dims = (((0,), (0,)), ((), ()))
    dot = functools.partial(lax.dot_general, dimension_numbers=dims, preferred_element_type=jnp.float32)
    return dot(left[0], right[0]) + (dot(left[0], right[1]) + dot(left[1], right[0]))


def lane_gather(table, index):
    return jnp.take_along_axis(table, index, axis=1)


def row8(row):
    return jnp.broadcast_to(row, (8, LANES))


def orient_kernel(field_ref, signs_ref, map_ref, oriented_ref, traces_ref):
    edges = signs_ref.shape[0]
    rows = lax.broadcasted_iota(jnp.int32, (40, edges), 0)
    edge = lax.broadcasted_iota(jnp.int32, (40, edges), 1)
    picks = ((rows < 36) & (rows % 3 != 1) & (rows // 3 == edge)).astype(jnp.bfloat16)
    shifted = (signs_ref[...] - 1).astype(jnp.float32).astype(jnp.bfloat16)
    factor = 1.0 + jnp.dot(picks, shifted, preferred_element_type=jnp.float32)
    oriented_ref[0:40, :] = field_ref[0:40, :] * factor
    oriented_ref[40:, :] = field_ref[40:, :]
    traces_ref[...] = product3(split3(map_ref[...]), split3(oriented_ref[...]))


def orient(field, edge_signs, trace_map):
    dofs, count = field.shape
    edges = edge_signs.shape[0]
    block = min(count, 512)
    return pl.pallas_call(
        orient_kernel,
        grid=(count // block,),
        in_specs=[
            pl.BlockSpec((dofs, block), lambda i: (0, i)),
            pl.BlockSpec((edges, block), lambda i: (0, i)),
            pl.BlockSpec((dofs, dofs), lambda i: (0, 0)),
        ],
        out_specs=[pl.BlockSpec((dofs, block), lambda i: (0, i))] * 2,
        out_shape=[jax.ShapeDtypeStruct((dofs, count), jnp.float32)] * 2,
        compiler_params=pltpu.CompilerParams(vmem_limit_bytes=VMEM_LIMIT),
        cost_estimate=pl.CostEstimate(flops=2 * dofs * dofs * count * 3, bytes_accessed=12 * dofs * count, transcendentals=0),
        name="orient",
    )(field, edge_signs, trace_map)


def quarter_swap(parts, lane):
    upper = (lane & 64) != 0
    odd = (lane & 32) != 0
    a0, a1, a2, a3 = parts
    b0 = jnp.where(upper, pltpu.roll(a2, 64, 1), a0)
    b2 = jnp.where(upper, a2, pltpu.roll(a0, 64, 1))
    b1 = jnp.where(upper, pltpu.roll(a3, 64, 1), a1)
    b3 = jnp.where(upper, a3, pltpu.roll(a1, 64, 1))
    c0 = jnp.where(odd, pltpu.roll(b1, 32, 1), b0)
    c1 = jnp.where(odd, b1, pltpu.roll(b0, 96, 1))
    c2 = jnp.where(odd, pltpu.roll(b3, 32, 1), b2)
    c3 = jnp.where(odd, b3, pltpu.roll(b2, 96, 1))
    return c0, c1, c2, c3


def pack_kernel(oriented_ref, scale_ref, owner_ref, payload_ref, high_ref, low_ref):
    tiles = owner_ref.shape[1] // LANES
    groups = payload_ref.shape[0] // 4
    bf = jnp.bfloat16
    sub = lax.broadcasted_iota(jnp.int32, (LANES, LANES), 0)
    lane_full = lax.broadcasted_iota(jnp.int32, (LANES, LANES), 1)
    upto = (sub <= lane_full).astype(jnp.float32).astype(bf)
    ones = jnp.ones((LANES, LANES), bf)
    before = jnp.zeros((LANES, LANES), jnp.float32)
    nt = (((1,), (1,)), ((), ()))
    table = jnp.zeros((3 * groups, LANES), jnp.float32)
    for tile in range(tiles):
        owner = owner_ref[:, tile * LANES : (tile + 1) * LANES]
        onehot = sub == owner
        hot = onehot.astype(jnp.float32)
        hot16 = hot.astype(bf)
        ordinal = before + jnp.dot(hot16, upto, preferred_element_type=jnp.float32) - 1.0
        rank = jnp.sum(jnp.where(onehot, ordinal, 0.0), axis=0, keepdims=True)
        before = before + jnp.dot(hot16, ones, preferred_element_type=jnp.float32)
        place = (owner & 3) * 32 + rank.astype(jnp.int32)
        landing = (sub == place).astype(jnp.float32).astype(bf)
        group = lax.broadcasted_iota(jnp.int32, (groups, LANES), 0) == (owner >> 2)
        groupf = group.astype(jnp.float32)
        lane_row = lax.broadcasted_iota(jnp.int32, (groups, LANES), 1).astype(jnp.float32)
        left = jnp.concatenate([groupf, groupf * lane_row, groupf * float(tile)], axis=0).astype(bf)
        table = table + lax.dot_general(left, landing, nt, preferred_element_type=jnp.float32)
    found = table[:groups]
    high_ref[...] = jnp.where(found > 0.5, table[2 * groups :], -1.0).astype(jnp.int32)
    low_ref[...] = table[groups : 2 * groups].astype(jnp.int32)

    lane = lax.broadcasted_iota(jnp.int32, (8, LANES), 1)
    rows = oriented_ref.shape[0] // 8

    def one_group(step, carry):
        high = row8(high_ref[pl.ds(step, 1), :])
        low = row8(low_ref[pl.ds(step, 1), :])
        taken = [jnp.zeros((8, LANES), jnp.float32) for _ in range(rows + 1)]
        for tile in range(tiles):
            hit = high == tile
            cols = slice(tile * LANES, (tile + 1) * LANES)
            for r in range(rows + 1):
                source = oriented_ref[8 * r : 8 * r + 8, cols] if r < rows else scale_ref[:, cols]
                taken[r] = jnp.where(hit, lane_gather(source, low), taken[r])
        taken.append(jnp.zeros((8, LANES), jnp.float32))
        for i in range(len(taken) // 4):
            outs = quarter_swap(taken[4 * i : 4 * i + 4], lane)
            for q in range(4):
                payload_ref[4 * step + q, 8 * i : 8 * i + 8, :] = outs[q]
        return carry

    lax.fori_loop(0, groups, one_group, 0)


def pack(oriented, scale, owner, devices):
    dofs, count = oriented.shape
    depth = 8 * ((dofs // 8 + 1 + 3) // 4)
    groups = devices // 4
    whole = pl.BlockSpec(memory_space=pltpu.VMEM)
    return pl.pallas_call(
        pack_kernel,
        in_specs=[whole] * 3,
        out_specs=whole,
        out_shape=jax.ShapeDtypeStruct((devices, depth, LANES), jnp.float32),
        scratch_shapes=[pltpu.VMEM((groups, LANES), jnp.int32), pltpu.VMEM((groups, LANES), jnp.int32)],
        compiler_params=pltpu.CompilerParams(vmem_limit_bytes=VMEM_LIMIT),
        cost_estimate=pl.CostEstimate(flops=10**9, bytes_accessed=8 * 10**6, transcendentals=0),
        name="pack",
    )(oriented, scale, owner)


def jump_kernel(base_ref, own_ref, left_ref, right_ref, nbrs_ref, size_ref, out_ref):
    count = own_ref.shape[1]
    tiles = count // LANES
    width = own_ref.shape[0] // 6
    vecs = width // 8
    base = base_ref[0]
    sides = (left_ref, own_ref, right_ref)

    def one_tile(step, carry):
        cols = pl.ds(pl.multiple_of(step * LANES, LANES), LANES)
        total = jnp.zeros((8, LANES), jnp.float32)
        for face in range(6):
            other = face ^ 1
            nbr = row8(nbrs_ref[face : face + 1, cols])
            spot = jnp.where(nbr >= 0, nbr - base, -LANES)
            high = spot >> 7
            low = spot & (LANES - 1)
            got = [jnp.zeros((8, LANES), jnp.float32) for _ in range(vecs)]
            for s, side in enumerate(sides):
                for tile in range(tiles):
                    hit = high == (s * tiles + tile)
                    for v in range(vecs):
                        r = other * width + 8 * v
                        source = side[r : r + 8, tile * LANES : (tile + 1) * LANES]
                        got[v] = jnp.where(hit, lane_gather(source, low), got[v])
            for v in range(vecs):
                r = face * width + 8 * v
                jump = own_ref[r : r + 8, cols] - got[v]
                total = total + jump * jump
        squares = jnp.sum(total, axis=0, keepdims=True)
        out_ref[:, cols] = jnp.sqrt(size_ref[:, cols] * (squares / (6 * width)) + 1e-06)
        return carry

    lax.fori_loop(0, tiles, one_tile, 0)


def jumps(base, own, left, right, nbrs, size):
    whole = pl.BlockSpec(memory_space=pltpu.VMEM)
    count = own.shape[1]
    return pl.pallas_call(
        jump_kernel,
        in_specs=[pl.BlockSpec(memory_space=pltpu.SMEM)] + [whole] * 5,
        out_specs=whole,
        out_shape=jax.ShapeDtypeStruct((1, count), jnp.float32),
        compiler_params=pltpu.CompilerParams(vmem_limit_bytes=VMEM_LIMIT),
        cost_estimate=pl.CostEstimate(flops=10**9, bytes_accessed=4 * 10**6, transcendentals=0),
        name="jumps",
    )(base, own, left, right, nbrs, size)


def apply_kernel(received_ref, stiffness_ref, mass_ref, migrated_ref, applied_ref, scale_ref):
    lane = lax.broadcasted_iota(jnp.int32, (8, LANES), 1)
    dofs = migrated_ref.shape[0]
    rows = dofs // 8
    for t in range(received_ref.shape[0] // 4):
        cols = slice(t * LANES, (t + 1) * LANES)
        for i in range(received_ref.shape[1] // 8):
            outs = quarter_swap([received_ref[4 * t + q, 8 * i : 8 * i + 8, :] for q in range(4)], lane)
            for q in range(4):
                r = 4 * i + q
                if r < rows:
                    migrated_ref[8 * r : 8 * r + 8, cols] = outs[q]
                elif r == rows:
                    scale_ref[:, cols] = outs[q]
    right = split3(migrated_ref[...])
    first = product3(split3(stiffness_ref[...]), right)
    second = product3(split3(mass_ref[...]), right)
    applied_ref[...] = scale_ref[0:1, :] * first + scale_ref[1:2, :] * second


def apply_received(received, stiffness, mass):
    devices, depth, _ = received.shape
    dofs = stiffness.shape[0]
    per = 16
    block = per * 32
    return pl.pallas_call(
        apply_kernel,
        grid=(devices // per,),
        in_specs=[
            pl.BlockSpec((per, depth, LANES), lambda i: (i, 0, 0)),
            pl.BlockSpec((dofs, dofs), lambda i: (0, 0)),
            pl.BlockSpec((dofs, dofs), lambda i: (0, 0)),
        ],
        out_specs=[pl.BlockSpec((dofs, block), lambda i: (0, i))] * 2,
        out_shape=[jax.ShapeDtypeStruct((dofs, devices * 32), jnp.float32)] * 2,
        scratch_shapes=[pltpu.VMEM((8, block), jnp.float32)],
        compiler_params=pltpu.CompilerParams(vmem_limit_bytes=VMEM_LIMIT),
        cost_estimate=pl.CostEstimate(flops=10**9, bytes_accessed=8 * 10**6, transcendentals=0),
        name="apply",
    )(received, stiffness, mass)


def body(field, edge_signs, face_nbrs, elem_size, mu_inv, permittivity, new_owner, trace_map, stiffness, mass):
    count = field.shape[1]
    devices = lax.axis_size(AXES)
    me = lax.axis_index(AXES)
    oriented, traces = orient(field, edge_signs, trace_map)
    left = lax.ppermute(traces, AXES, [(i, i + 1) for i in range(devices - 1)])
    right = lax.ppermute(traces, AXES, [(i + 1, i) for i in range(devices - 1)])
    scale = jnp.concatenate(
        [mu_inv.reshape(1, count), permittivity.reshape(1, count), jnp.zeros((6, count), jnp.float32)], axis=0
    )
    payload = pack(oriented, scale, new_owner.reshape(1, count), devices)
    received = lax.all_to_all(payload, AXES, split_axis=0, concat_axis=0, tiled=True)
    base = ((me - 1) * count).astype(jnp.int32).reshape(1)
    indicators = jumps(base, traces, left, right, face_nbrs, elem_size.reshape(1, count))
    migrated, applied = apply_received(received, stiffness, mass)
    return indicators.reshape(count), migrated, applied


def solution(mesh):
    flat = P(AXES)
    wide = P(None, AXES)
    in_specs = (wide, wide, wide, flat, flat, flat, P(AXES, None), P(), P(), P())
    return jax.shard_map(body, mesh=mesh, in_specs=in_specs, out_specs=(flat, wide, wide), check_vma=False)
```

time: 154 us -> 123 us (0.80)
  the two profiles are of different devices: /device:TPU:26 before, /device:TPU:1 now
where the time goes in v1:
time: 123 us
  waiting for transfers between devices  49.6 us (40%)
  Pallas kernels  46 us (37%)
  starting transfers between devices  20.4 us (17%)
  local copies, waits for them, and re-layouts  5.46 us (4%)
    ppermute x1, waiting for transfers between devices, body(): right = lax.ppermute(traces, AXES, [(i + 1, i) for i in range(devices - 1)])  45.9 us
    pallas_call x1, Pallas kernels, pack(): pl.pallas_call(pack_kernel, in_specs=[whole] * 3, out_specs=whole, out_sh...  19.6 us
    pallas_call x1, Pallas kernels, jumps(): pl.pallas_call(jump_kernel, in_specs=[pl.BlockSpec(memory_space=pltpu.SME...  18.6 us
    all_to_all x1, starting transfers between devices, body(): lax.all_to_all(payload, AXES, split_axis=0, concat_axis=0, tiled=True)  11.5 us
    ppermute x1, starting transfers between devices, body(): right = lax.ppermute(traces, AXES, [(i + 1, i) for i in range(devices - 1)])  6.97 us
    pallas_call x1, Pallas kernels, apply_received(): pl.pallas_call(apply_kernel, grid=(devices // per,), in_specs=[pl.BlockSp...  5.89 us
    unnamed x20, local copies, waits for them, and re-layouts  5.38 us
    ppermute x1, waiting for transfers between devices, body(): left = lax.ppermute(traces, AXES, [(i, i + 1) for i in range(devices - 1)])  3.71 us
  transfers between devices with their start and end apart: 3, of which 2 were waited for; matrix products, arithmetic and copies ran while one was open for 0% of the time, Pallas kernels for 15%

profile of v1, /device:TPU:1, one launch (start us, length us, event | category | flops | bytes accessed | tf_op | source)
XLA Modules:
  0.0 122.9 jit_solution(17687709067244693667)
XLA Ops:
  0.6 0.0 copy-start.3
  0.7 0.1 pad.2.clone
  0.7 0.8 maximum_maximum_fusion.scale_ref
  1.5 0.0 copy-start
  1.5 1.3 %copy-done = f32[144,2048]{1,0:T(8,128)S(1)} copy-done((f32[144,2048]{1,0:T(8,128)S(1)}, f32[144,2048]{1,0:T(8,128)}, u32[]{:S(2)}) %copy-start) | copy-done | bytes 1179672
  2.8 0.0 copy-start.1
  2.8 0.9 copy-done.1
  3.7 0.0 copy-start.2
  3.7 0.9 copy-done.2
  4.6 1.8 %orient.1 = (f32[144,2048]{1,0:T(8,128)S(1)}, f32[144,2048]{1,0:T(8,128)S(1)}) custom-call(f32[144,2048]{1,0:T(8,128)S(1)} %copy-done, s32[12,2048]{1,0:T(8,128)S(1)} %copy-done.2, f32[144,144]{1,0:T(8,128)S(1)} %copy-done.1), custom_call_target="tpu_custom_call" | custom-call | flops 254803968 | bytes 3538944 | tf_op jit(solution)/shard_map/orient/pallas_call | solution.py:51
  6.5 0.0 copy-start.4
  6.5 1.0 copy-done.4
  7.5 0.0 copy-done.3
  7.5 19.6 %pack.1 = f32[128,40,128]{2,1,0:T(8,128)} custom-call(f32[144,2048]{1,0:T(8,128)S(1)} %get-tuple-element.8.oriented_ref, f32[8,2048]{1,0:T(8,128)S(1)} %maximum_maximum_fusion.scale_ref, s32[1,2048]{1,0:T(1,128)S(1)} %bitcast.6), custom_call_target="tpu_custom_call" | custom-call | flops 1000000000 | bytes 8000000 | tf_op jit(solution)/shard_map/pack/pallas_call | solution.py:140
  27.1 0.0 copy-start.8
  27.1 0.0 copy-start.9
  27.1 11.5 %all-to-all-start = ((f32[128,40,128]{2,1,0:T(8,128)}), f32[128,40,128]{2,1,0:T(8,128)S(1)}, u32[]{:S(2)}, u32[]{:S(2)}) async-start(f32[128,40,128]{2,1,0:T(8,128)} %pack.1), calls=%async_computation | async-start | bytes 5242880 | tf_op jit(solution)/shard_map/all_to_all | solution.py:255
  38.6 7.0 %collective-permute-start.1 = (f32[144,2048]{1,0:T(8,128)}, f32[144,2048]{1,0:T(8,128)}, u32[]{:S(2)}, u32[]{:S(2)}) collective-permute-start(f32[144,2048]{1,0:T(8,128)} %copy-done.4), channel_id=1, source_target_pairs={{1,0},{2,1},{3,2},{4,3},{5,4},{6,5},{7,6},{8,7},{9,8},{10,9},{11,1... | collective-permute-start | bytes 3538952 | tf_op jit(solution)/shard_map/ppermute | solution.py:250
  45.5 1.9 %collective-permute-start = (f32[144,2048]{1,0:T(8,128)}, f32[144,2048]{1,0:T(8,128)}, u32[]{:S(2)}, u32[]{:S(2)}) collective-permute-start(f32[144,2048]{1,0:T(8,128)} %copy-done.4), channel_id=1, source_target_pairs={{0,1},{1,2},{2,3},{3,4},{4,5},{5,6},{6,7},{7,8},{8,9},{9,10},{10,1... | collective-permute-start | bytes 3538952 | tf_op jit(solution)/shard_map/ppermute | solution.py:249
  47.5 45.9 %collective-permute-done.1.right_ref = f32[144,2048]{1,0:T(8,128)} collective-permute-done((f32[144,2048]{1,0:T(8,128)}, f32[144,2048]{1,0:T(8,128)}, u32[]{:S(2)}, u32[]{:S(2)}) %collective-permute-start.1) | collective-permute-done | bytes 1179680 | tf_op jit(solution)/shard_map/ppermute | solution.py:250
  93.4 3.7 %collective-permute-done.left_ref = f32[144,2048]{1,0:T(8,128)} collective-permute-done((f32[144,2048]{1,0:T(8,128)}, f32[144,2048]{1,0:T(8,128)}, u32[]{:S(2)}, u32[]{:S(2)}) %collective-permute-start) | collective-permute-done | bytes 1179680 | tf_op jit(solution)/shard_map/ppermute | solution.py:249
  97.1 0.0 copy-done.8
  97.1 0.0 copy-done.9
  97.1 0.0 copy-start.5
  97.1 1.3 %copy-done.5 = f32[144,2048]{1,0:T(8,128)S(1)} copy-done((f32[144,2048]{1,0:T(8,128)S(1)}, f32[144,2048]{1,0:T(8,128)}, u32[]{:S(2)}) %copy-start.5) | copy-done | bytes 1179672
  98.4 0.0 copy-start.6
  98.4 0.0 copy-start.7
  98.4 18.6 %jumps.1 = f32[1,2048]{1,0:T(1,128)} custom-call(s32[1]{0:T(128)} %bitcast.base_ref, f32[144,2048]{1,0:T(8,128)S(1)} %copy-done.5, f32[144,2048]{1,0:T(8,128)} %collective-permute-done.left_ref, f32[144,2048]{1,0:T(8,128)} %collective-permute-done.1.right_ref, s32[6,2048]{1,0:T(8,128)S(1)} %copy-done.8, f32[1,2048]{1,0:T(1,128)S(1)} %bitcast.7), custom_call_target="tpu_custom_call" | custom-call | flops 1000000000 | bytes 4000000 | tf_op jit(solution)/shard_map/jumps/pallas_call | solution.py:191
  117.0 0.0 all-to-all-done.received_ref
  117.0 0.0 copy-done.6
  117.0 0.0 copy-done.7
  117.0 5.9 %apply.1 = (f32[144,4096]{1,0:T(8,128)}, f32[144,4096]{1,0:T(8,128)}) custom-call(f32[128,40,128]{2,1,0:T(8,128)S(1)} %all-to-all-done.received_ref, f32[144,144]{1,0:T(8,128)S(1)} %copy-done.6, f32[144,144]{1,0:T(8,128)S(1)} %copy-done.7), custom_call_target="tpu_custom_call" | custom-call | flops 1000000000 | bytes 8000000 | tf_op jit(solution)/shard_map/apply/pallas_call | solution.py:227
  (1 shorter events, 0.0 us)
Async XLA Ops:
  0.6 6.8 %copy-start.3 = (s32[2048,1]{0,1:T(1,128)S(1)}, s32[2048,1]{0,1:T(1,128)}, u32[]{:S(2)}) copy-start(s32[2048,1]{0,1:T(1,128)} %param.16) | copy-start | bytes 24580
  1.5 1.3 %copy-start = (f32[144,2048]{1,0:T(8,128)S(1)}, f32[144,2048]{1,0:T(8,128)}, u32[]{:S(2)}) copy-start(f32[144,2048]{1,0:T(8,128)} %field_ref.1) | copy-start | bytes 3538948
  2.8 0.9 copy-start.1
  3.7 0.9 copy-start.2
  6.5 1.0 copy-start.4
  27.1 70.0 %copy-start.8 = (s32[6,2048]{1,0:T(8,128)S(1)}, s32[6,2048]{1,0:T(8,128)}, u32[]{:S(2)}) copy-start(s32[6,2048]{1,0:T(8,128)} %nbrs_ref.1) | copy-start | bytes 147460
  27.1 70.0 %copy-start.9 = (f32[2048]{0:T(1024)S(1)}, f32[2048]{0:T(1024)}, u32[]{:S(2)}) copy-start(f32[2048]{0:T(1024)} %param.13) | copy-start | bytes 24580
  27.1 90.0 %all-to-all-start = ((f32[128,40,128]{2,1,0:T(8,128)}), f32[128,40,128]{2,1,0:T(8,128)S(1)}, u32[]{:S(2)}, u32[]{:S(2)}) async-start(f32[128,40,128]{2,1,0:T(8,128)} %pack.1), calls=%async_computation | async-start | bytes 5242880 | tf_op jit(solution)/shard_map/all_to_all | solution.py:255
  38.6 54.8 %collective-permute-start.1 = (f32[144,2048]{1,0:T(8,128)}, f32[144,2048]{1,0:T(8,128)}, u32[]{:S(2)}, u32[]{:S(2)}) collective-permute-start(f32[144,2048]{1,0:T(8,128)} %copy-done.4), channel_id=1, source_target_pairs={{1,0},{2,1},{3,2},{4,3},{5,4},{6,5},{7,6},{8,7},{9,8},{10,9},{11,1... | collective-permute-start | bytes 3538952 | tf_op jit(solution)/shard_map/ppermute | solution.py:250
  45.5 51.6 %collective-permute-start = (f32[144,2048]{1,0:T(8,128)}, f32[144,2048]{1,0:T(8,128)}, u32[]{:S(2)}, u32[]{:S(2)}) collective-permute-start(f32[144,2048]{1,0:T(8,128)} %copy-done.4), channel_id=1, source_target_pairs={{0,1},{1,2},{2,3},{3,4},{4,5},{5,6},{6,7},{7,8},{8,9},{9,10},{10,1... | collective-permute-start | bytes 3538952 | tf_op jit(solution)/shard_map/ppermute | solution.py:249
  97.1 1.3 %copy-start.5 = (f32[144,2048]{1,0:T(8,128)S(1)}, f32[144,2048]{1,0:T(8,128)}, u32[]{:S(2)}) copy-start(f32[144,2048]{1,0:T(8,128)} %copy-done.4) | copy-start | bytes 3538948
  98.4 18.6 %copy-start.6 = (f32[144,144]{1,0:T(8,128)S(1)}, f32[144,144]{1,0:T(8,128)}, u32[]{:S(2)}) copy-start(f32[144,144]{1,0:T(8,128)} %stiffness_ref.1) | copy-start | bytes 248836
  98.4 18.6 %copy-start.7 = (f32[144,144]{1,0:T(8,128)S(1)}, f32[144,144]{1,0:T(8,128)}, u32[]{:S(2)}) copy-start(f32[144,144]{1,0:T(8,128)} %mass_ref.1) | copy-start | bytes 248836

commit v2 on v1

v2 whole, which is shorter than its diff:
```python
import functools

import jax
import jax.numpy as jnp
from jax import lax
from jax.experimental import pallas as pl
from jax.experimental.pallas import tpu as pltpu
from jax.sharding import PartitionSpec as P

AXES = ("gx", "yz")
LANES = 128
VMEM_LIMIT = 60 << 20


def split3(value):
    high = value.astype(jnp.bfloat16)
    low = (value - high.astype(jnp.float32)).astype(jnp.bfloat16)
    return high, low


def product3(left, right):
    dims = (((0,), (0,)), ((), ()))
    dot = functools.partial(lax.dot_general, dimension_numbers=dims, preferred_element_type=jnp.float32)
    return dot(left[0], right[0]) + (dot(left[0], right[1]) + dot(left[1], right[0]))


def lane_gather(table, index):
    return jnp.take_along_axis(table, index, axis=1)


def row8(row):
    return jnp.broadcast_to(row, (8, LANES))


def quarter_swap(parts, lane):
    upper = (lane & 64) != 0
    odd = (lane & 32) != 0
    a0, a1, a2, a3 = parts
    b0 = jnp.where(upper, pltpu.roll(a2, 64, 1), a0)
    b2 = jnp.where(upper, a2, pltpu.roll(a0, 64, 1))
    b1 = jnp.where(upper, pltpu.roll(a3, 64, 1), a1)
    b3 = jnp.where(upper, a3, pltpu.roll(a1, 64, 1))
    c0 = jnp.where(odd, pltpu.roll(b1, 32, 1), b0)
    c1 = jnp.where(odd, b1, pltpu.roll(b0, 96, 1))
    c2 = jnp.where(odd, pltpu.roll(b3, 32, 1), b2)
    c3 = jnp.where(odd, b3, pltpu.roll(b2, 96, 1))
    return c0, c1, c2, c3


MESH = pl.DeviceIdType.MESH
CHUNKS = 4


def bit(k, n):
    return lax.rem(lax.div(k, 2**n), 2)


def offsets(k):
    return bit(k, 1) + 2 * bit(k, 3), bit(k, 4), bit(k, 0) + 2 * bit(k, 2)


def exchange_kernel(
    field_ref, signs_ref, nbrs_ref, mu_ref, eps_ref, owner_ref, map_ref,
    squares_ref, received_ref,
    oriented, traces, left, right, signs, nbrs, mu, eps, owner, tmap, scale, high_ref, low_ref, payload, bundle,
    in_sem, halo_send, halo_recv, a_send, a_recv, f_send, f_recv, own_sem,
):
    gx = lax.axis_index("gx")
    yz = lax.axis_index("yz")
    gx_size = lax.axis_size("gx")
    yz_size = lax.axis_size("yz")
    devices = gx_size * yz_size
    me = gx * yz_size + yz
    z, c = lax.div(gx, 2), lax.rem(gx, 2)
    y, x = lax.div(yz, 4), lax.rem(yz, 4)
    plane = gx * 4 + y
    planes = devices // 4
    dofs, count = oriented.shape
    depth = payload.shape[1]
    block = count // CHUNKS

    def at(index):
        return (lax.div(index, yz_size), lax.rem(index, yz_size))

    def in_plane(p):
        return (lax.div(p, 4), lax.rem(p, 4) * 4 + x)

    def target(k):
        oz, oc, oy = offsets(k)
        return (lax.rem(z + oz, 4) * 2 + lax.rem(c + oc, 2)) * 4 + lax.rem(y + oy, 4)

    def source(k):
        oz, oc, oy = offsets(k)
        return (lax.rem(z + 4 - oz, 4) * 2 + lax.rem(c + 2 - oc, 2)) * 4 + lax.rem(y + 4 - oy, 4)

    ahead = at(lax.rem(me + 1, devices))
    behind = at(lax.rem(me + devices - 1, devices))

    loads = [
        pltpu.make_async_copy(signs_ref, signs, in_sem.at[0]),
        pltpu.make_async_copy(map_ref, tmap, in_sem.at[1]),
    ]
    fields = []
    for part in range(CHUNKS):
        cols = pl.ds(part * block, block)
        fields.append(pltpu.make_async_copy(field_ref.at[:, cols], oriented.at[:, cols], in_sem.at[2 + part]))
    later = [
        pltpu.make_async_copy(s, d, in_sem.at[2 + CHUNKS + i])
        for i, (s, d) in enumerate(((owner_ref, owner), (mu_ref, mu), (eps_ref, eps), (nbrs_ref, nbrs)))
    ]
    for copy in loads + fields + later:
        copy.start()

    barrier = pltpu.get_barrier_semaphore()

    def greet(k, carry):
        pl.semaphore_signal(barrier, inc=1, device_id=in_plane(target(k)), device_id_type=MESH)
        return carry

    lax.fori_loop(1, planes, greet, 0)
    for step in range(1, 4):
        pl.semaphore_signal(barrier, inc=1, device_id=(gx, y * 4 + lax.rem(x + step, 4)), device_id_type=MESH)
    pl.semaphore_signal(barrier, inc=1, device_id=ahead, device_id_type=MESH)
    pl.semaphore_signal(barrier, inc=1, device_id=behind, device_id_type=MESH)

    edges = signs.shape[0]
    rows = lax.broadcasted_iota(jnp.int32, (40, edges), 0)
    edge = lax.broadcasted_iota(jnp.int32, (40, edges), 1)
    picks = ((rows < 36) & (rows % 3 != 1) & (rows // 3 == edge)).astype(jnp.bfloat16)

    def halo(part):
        cols = pl.ds(part * block, block)
        return [
            pltpu.make_async_remote_copy(
                src_ref=traces.at[:, cols], dst_ref=side.at[:, cols], send_sem=halo_send.at[i, part],
                recv_sem=halo_recv.at[i, part], device_id=peer, device_id_type=MESH,
            )
            for i, (side, peer) in enumerate(((left, ahead), (right, behind)))
        ]

    for copy in loads:
        copy.wait()
    map_parts = split3(tmap[...])
    for part in range(CHUNKS):
        cols = slice(part * block, (part + 1) * block)
        fields[part].wait()
        shifted = (signs[:, cols] - 1).astype(jnp.float32).astype(jnp.bfloat16)
        factor = 1.0 + jnp.dot(picks, shifted, preferred_element_type=jnp.float32)
        oriented[0:40, cols] = oriented[0:40, cols] * factor
        traces[:, cols] = product3(map_parts, split3(oriented[:, cols]))
        if part == 1:
            pl.semaphore_wait(barrier, planes - 1 + 3 + 2)
        if part >= 1:
            for copy in halo(part - 1):
                copy.start()
    for copy in later:
        copy.wait()

    tiles = count // LANES
    bf = jnp.bfloat16
    sub = lax.broadcasted_iota(jnp.int32, (LANES, LANES), 0)
    lane_full = lax.broadcasted_iota(jnp.int32, (LANES, LANES), 1)
    upto = (sub <= lane_full).astype(jnp.float32).astype(bf)
    ones = jnp.ones((LANES, LANES), bf)
    before = jnp.zeros((LANES, LANES), jnp.float32)
    nt = (((1,), (1,)), ((), ()))
    table = jnp.zeros((3 * planes, LANES), jnp.float32)
    sub8 = lax.broadcasted_iota(jnp.int32, (8, LANES), 0)
    for tile in range(tiles):
        cols = slice(tile * LANES, (tile + 1) * LANES)
        scale[:, cols] = jnp.where(sub8 == 0, row8(mu[:, cols]), jnp.where(sub8 == 1, row8(eps[:, cols]), 0.0))
        own = owner[:, cols]
        onehot = sub == own
        hot = onehot.astype(jnp.float32)
        hot16 = hot.astype(bf)
        ordinal = before + jnp.dot(hot16, upto, preferred_element_type=jnp.float32) - 1.0
        rank = jnp.sum(jnp.where(onehot, ordinal, 0.0), axis=0, keepdims=True)
        before = before + jnp.dot(hot16, ones, preferred_element_type=jnp.float32)
        place = (own & 3) * 32 + rank.astype(jnp.int32)
        landing = (sub == place).astype(jnp.float32).astype(bf)
        group = lax.broadcasted_iota(jnp.int32, (planes, LANES), 0) == (own >> 2)
        groupf = group.astype(jnp.float32)
        lane_row = lax.broadcasted_iota(jnp.int32, (planes, LANES), 1).astype(jnp.float32)
        parts = jnp.concatenate([groupf, groupf * lane_row, groupf * float(tile)], axis=0).astype(bf)
        table = table + lax.dot_general(parts, landing, nt, preferred_element_type=jnp.float32)
    found = table[:planes]
    high_ref[...] = jnp.where(found > 0.5, table[2 * planes :], -1.0).astype(jnp.int32)
    low_ref[...] = table[planes : 2 * planes].astype(jnp.int32)
    for copy in halo(CHUNKS - 1):
        copy.start()

    lane = lax.broadcasted_iota(jnp.int32, (8, LANES), 1)
    vectors = dofs // 8

    def pack_group(k):
        t = target(k)
        high = row8(high_ref[pl.ds(t, 1), :])
        low = row8(low_ref[pl.ds(t, 1), :])
        taken = [jnp.zeros((8, LANES), jnp.float32) for _ in range(vectors + 1)]
        for tile in range(tiles):
            hit = high == tile
            cols = slice(tile * LANES, (tile + 1) * LANES)
            for r in range(vectors + 1):
                piece = oriented[8 * r : 8 * r + 8, cols] if r < vectors else scale[:, cols]
                taken[r] = jnp.where(hit, lane_gather(piece, low), taken[r])
        while len(taken) % 4:
            taken.append(jnp.zeros((8, LANES), jnp.float32))
        for i in range(len(taken) // 4):
            outs = quarter_swap(taken[4 * i : 4 * i + 4], lane)
            for q in range(4):
                payload[4 * t + q, 8 * i : 8 * i + 8, :] = outs[q]

    def send_group(k):
        t = target(k)
        pltpu.make_async_remote_copy(
            src_ref=payload.at[pl.ds(4 * t, 4)], dst_ref=bundle.at[pl.ds(4 * plane, 4)], send_sem=a_send,
            recv_sem=a_recv.at[plane], device_id=in_plane(t), device_id_type=MESH,
        ).start()

    def pack_step(k, carry):
        pack_group(k)

        @pl.when(k > 1)
        def _():
            send_group(k - 1)

        return carry

    lax.fori_loop(1, planes, pack_step, 0)
    pack_group(0)
    send_group(planes - 1)

    def forward(origin, s):
        for step in range(1, 4):
            xd = lax.rem(x + step, 4)
            pltpu.make_async_remote_copy(
                src_ref=origin.at[4 * s + xd], dst_ref=received_ref.at[4 * s + x], send_sem=f_send, recv_sem=f_recv,
                device_id=(gx, y * 4 + xd), device_id_type=MESH,
            ).start()
        pltpu.make_async_copy(origin.at[4 * s + x], received_ref.at[4 * s + x], own_sem).start()

    def forward_step(k):
        s = source(k)
        pltpu.make_async_remote_copy(
            src_ref=payload.at[pl.ds(4 * s, 4)], dst_ref=bundle.at[pl.ds(4 * s, 4)], send_sem=a_send,
            recv_sem=a_recv.at[s], device_id=ahead, device_id_type=MESH,
        ).wait_recv()
        forward(bundle, s)

    early = planes // 2 + 1

    def early_step(k, carry):
        forward_step(k)
        return carry

    lax.fori_loop(1, early, early_step, 0)
    forward(payload, plane)

    for part in range(CHUNKS):
        for copy in halo(part):
            copy.wait_recv()

    width = dofs // 6
    vecs = width // 8
    base = (me - 1) * count
    sides = (left, traces, right)

    def jump_tile(step, carry):
        @pl.when(step + early < planes)
        def _():
            forward_step(step + early)

        cols = pl.ds(pl.multiple_of(step * LANES, LANES), LANES)
        total = jnp.zeros((8, LANES), jnp.float32)
        for face in range(6):
            other = face ^ 1
            nbr = row8(nbrs[face : face + 1, cols])
            spot = jnp.where(nbr >= 0, nbr - base, -LANES)
            high = spot >> 7
            low = spot & (LANES - 1)
            got = [jnp.zeros((8, LANES), jnp.float32) for _ in range(vecs)]
            for i, side in enumerate(sides):
                for tile in range(tiles):
                    hit = high == (i * tiles + tile)
                    for v in range(vecs):
                        r = other * width + 8 * v
                        piece = side[r : r + 8, tile * LANES : (tile + 1) * LANES]
                        got[v] = jnp.where(hit, lane_gather(piece, low), got[v])
            for v in range(vecs):
                r = face * width + 8 * v
                jump = traces[r : r + 8, cols] - got[v]
                total = total + jump * jump
        squares_ref[:, cols] = jnp.sum(total, axis=0, keepdims=True)
        return carry

    lax.fori_loop(0, tiles, jump_tile, 0)

    for part in range(CHUNKS):
        for copy in halo(part):
            copy.wait_send()
    sent = 4 * (planes - 1)
    pltpu.make_async_remote_copy(
        src_ref=payload.at[pl.ds(0, sent)], dst_ref=bundle.at[pl.ds(0, sent)], send_sem=a_send, recv_sem=a_recv.at[0],
        device_id=ahead, device_id_type=MESH,
    ).wait_send()
    moved = 3 * planes
    along = pltpu.make_async_remote_copy(
        src_ref=bundle.at[pl.ds(0, moved)], dst_ref=received_ref.at[pl.ds(0, moved)], send_sem=f_send, recv_sem=f_recv,
        device_id=ahead, device_id_type=MESH,
    )
    along.wait_send()
    along.wait_recv()
    pltpu.make_async_copy(bundle.at[pl.ds(0, planes)], received_ref.at[pl.ds(0, planes)], own_sem).wait()


def exchange(field, edge_signs, face_nbrs, mu, eps, owner, trace_map, devices):
    dofs, count = field.shape
    planes = devices // 4
    depth = 8 * ((dofs // 8 + 1 + 3) // 4)
    anywhere = pl.BlockSpec(memory_space=pl.ANY)
    wide = pltpu.VMEM((dofs, count), jnp.float32)
    blocks = pltpu.VMEM((devices, depth, LANES), jnp.float32)
    row = pltpu.VMEM((1, count), jnp.float32)
    dma = pltpu.SemaphoreType.DMA
    return pl.pallas_call(
        exchange_kernel,
        in_specs=[anywhere] * 7,
        out_specs=[pl.BlockSpec(memory_space=pltpu.VMEM), anywhere],
        out_shape=[
            jax.ShapeDtypeStruct((1, count), jnp.float32),
            jax.ShapeDtypeStruct((devices, depth, LANES), jnp.float32),
        ],
        scratch_shapes=[
            wide, wide, wide, wide,
            pltpu.VMEM(edge_signs.shape, jnp.int32),
            pltpu.VMEM(face_nbrs.shape, jnp.int32),
            row, row, pltpu.VMEM((1, count), jnp.int32),
            pltpu.VMEM(trace_map.shape, jnp.float32),
            pltpu.VMEM((8, count), jnp.float32),
            pltpu.VMEM((planes, LANES), jnp.int32),
            pltpu.VMEM((planes, LANES), jnp.int32),
            blocks, blocks,
            dma((CHUNKS + 6,)), dma((2, CHUNKS)), dma((2, CHUNKS)), dma, dma((planes,)), dma, dma, dma,
        ],
        compiler_params=pltpu.CompilerParams(collective_id=0, has_side_effects=True, vmem_limit_bytes=VMEM_LIMIT),
        name="exchange",
    )(field, edge_signs, face_nbrs, mu, eps, owner, trace_map)


def apply_kernel(
    received_ref, stiffness_ref, mass_ref, squares_ref, size_ref, migrated_ref, applied_ref, out_ref, scale_ref
):
    @pl.when(pl.program_id(0) == 0)
    def _():
        out_ref[...] = jnp.sqrt(size_ref[...] * (squares_ref[...] / stiffness_ref.shape[0]) + 1e-06)

    lane = lax.broadcasted_iota(jnp.int32, (8, LANES), 1)
    dofs = migrated_ref.shape[0]
    rows = dofs // 8
    for t in range(received_ref.shape[0] // 4):
        cols = slice(t * LANES, (t + 1) * LANES)
        for i in range(received_ref.shape[1] // 8):
            outs = quarter_swap([received_ref[4 * t + q, 8 * i : 8 * i + 8, :] for q in range(4)], lane)
            for q in range(4):
                r = 4 * i + q
                if r < rows:
                    migrated_ref[8 * r : 8 * r + 8, cols] = outs[q]
                elif r == rows:
                    scale_ref[:, cols] = outs[q]
    right = split3(migrated_ref[...])
    first = product3(split3(stiffness_ref[...]), right)
    second = product3(split3(mass_ref[...]), right)
    applied_ref[...] = scale_ref[0:1, :] * first + scale_ref[1:2, :] * second


def apply_received(received, stiffness, mass, squares, size):
    devices, depth, _ = received.shape
    dofs = stiffness.shape[0]
    per = 16
    block = per * 32
    return pl.pallas_call(
        apply_kernel,
        grid=(devices // per,),
        in_specs=[
            pl.BlockSpec((per, depth, LANES), lambda i: (i, 0, 0)),
            pl.BlockSpec((dofs, dofs), lambda i: (0, 0)),
            pl.BlockSpec((dofs, dofs), lambda i: (0, 0)),
            pl.BlockSpec(squares.shape, lambda i: (0, 0)),
            pl.BlockSpec(squares.shape, lambda i: (0, 0)),
        ],
        out_specs=[pl.BlockSpec((dofs, block), lambda i: (0, i))] * 2 + [pl.BlockSpec(squares.shape, lambda i: (0, 0))],
        out_shape=[jax.ShapeDtypeStruct((dofs, devices * 32), jnp.float32)] * 2
        + [jax.ShapeDtypeStruct(squares.shape, jnp.float32)],
        scratch_shapes=[pltpu.VMEM((8, block), jnp.float32)],
        compiler_params=pltpu.CompilerParams(vmem_limit_bytes=VMEM_LIMIT),
        cost_estimate=pl.CostEstimate(flops=10**9, bytes_accessed=8 * 10**6, transcendentals=0),
        name="apply",
    )(received, stiffness, mass, squares, size)


def body(field, edge_signs, face_nbrs, elem_size, mu_inv, permittivity, new_owner, trace_map, stiffness, mass):
    count = field.shape[1]
    devices = lax.axis_size(AXES)
    row = (1, count)
    squares, received = exchange(
        field, edge_signs, face_nbrs, mu_inv.reshape(row), permittivity.reshape(row), new_owner.reshape(row),
        trace_map, devices,
    )
    migrated, applied, indicators = apply_received(received, stiffness, mass, squares, elem_size.reshape(row))
    return indicators.reshape(count), migrated, applied


def solution(mesh):
    flat = P(AXES)
    wide = P(None, AXES)
    in_specs = (wide, wide, wide, flat, flat, flat, P(AXES, None), P(), P(), P())
    return jax.shard_map(body, mesh=mesh, in_specs=in_specs, out_specs=(flat, wide, wide), check_vma=False)
```

time: 123 us -> 83 us (0.67)
  the two profiles are of different devices: /device:TPU:1 before, /device:TPU:26 now
where the time goes in v2:
time: 83 us; the launch traced here: 81.5 us
  Pallas kernels  80.9 us (97%)
    pallas_call x1, Pallas kernels, exchange(): pl.pallas_call(exchange_kernel, in_specs=[anywhere] * 7, out_specs=[pl.Bl...  72.6 us
    pallas_call x1, Pallas kernels, apply_received(): pl.pallas_call(apply_kernel, grid=(devices // per,), in_specs=[pl.BlockSp...  8.24 us

profile of v2, /device:TPU:26, one launch (start us, length us, event | category | flops | bytes accessed | tf_op | source)
XLA Modules:
  0.0 81.5 jit_solution(10724868262823418082)
XLA Ops:
  0.6 72.6 %exchange.1 = (f32[1,2048]{1,0:T(1,128)}, f32[128,40,128]{2,1,0:T(8,128)}) custom-call(f32[144,2048]{1,0:T(8,128)} %field_ref.1, s32[12,2048]{1,0:T(8,128)} %signs_ref.1, s32[6,2048]{1,0:T(8,128)} %nbrs_ref.1, f32[1,2048]{1,0:T(1,128)} %bitcast.5, f32[1,2048]{1,0:T(1,128)} %bitcast.6, s32[1,2048]{1,0:T(1,128)} %bitcast.7, f32[144,144]{1,0:T(8,128)} %map_ref.1), custom_call_target="tpu_custom_call" | custom-call | tf_op jit(solution)/shard_map/exchange/pallas_call | solution.py:325
  73.3 8.2 %apply.1 = (f32[144,4096]{1,0:T(8,128)}, f32[144,4096]{1,0:T(8,128)}, f32[1,2048]{1,0:T(1,128)}) custom-call(f32[128,40,128]{2,1,0:T(8,128)} %get-tuple-element.8.received_ref, f32[144,144]{1,0:T(8,128)} %stiffness_ref.1, f32[144,144]{1,0:T(8,128)} %mass_ref.1, f32[1,2048]{1,0:T(1,128)} %get-tuple-element.9.squares_ref, f32[1,2048]{1,0:T(1,128)} %bitcast.8), custom_call_target="tpu_custom_call" | custom-call | flops 1000000000 | bytes 8000000 | tf_op jit(solution)/shard_map/apply/pallas_call | solution.py:381

commit v3 on v2

v3 whole, which is shorter than its diff:
```python
import functools

import jax
import jax.numpy as jnp
from jax import lax
from jax.experimental import pallas as pl
from jax.experimental.pallas import tpu as pltpu
from jax.sharding import PartitionSpec as P

AXES = ("gx", "yz")
LANES = 128
VMEM_LIMIT = 60 << 20


def split3(value):
    high = value.astype(jnp.bfloat16)
    low = (value - high.astype(jnp.float32)).astype(jnp.bfloat16)
    return high, low


def stacked_left(matrix):
    high, low = split3(jnp.transpose(matrix))
    return jnp.concatenate([high, high, low], axis=1)


def stacked_product(left, right):
    high, low = split3(right)
    return jnp.dot(left, jnp.concatenate([high, low, high], axis=0), preferred_element_type=jnp.float32)


def lane_gather(table, index):
    return jnp.take_along_axis(table, index, axis=1)


def row8(row):
    return jnp.broadcast_to(row, (8, LANES))


def quarter_swap(parts, lane):
    upper = (lane & 64) != 0
    odd = (lane & 32) != 0
    a0, a1, a2, a3 = parts
    b0 = jnp.where(upper, pltpu.roll(a2, 64, 1), a0)
    b2 = jnp.where(upper, a2, pltpu.roll(a0, 64, 1))
    b1 = jnp.where(upper, pltpu.roll(a3, 64, 1), a1)
    b3 = jnp.where(upper, a3, pltpu.roll(a1, 64, 1))
    c0 = jnp.where(odd, pltpu.roll(b1, 32, 1), b0)
    c1 = jnp.where(odd, b1, pltpu.roll(b0, 96, 1))
    c2 = jnp.where(odd, pltpu.roll(b3, 32, 1), b2)
    c3 = jnp.where(odd, b3, pltpu.roll(b2, 96, 1))
    return c0, c1, c2, c3


MESH = pl.DeviceIdType.MESH
CHUNKS = 4
MATRIX_FACES = (0, 1, 3, 5)


def bit(k, n):
    return lax.rem(lax.div(k, 2**n), 2)


def offsets(k):
    return bit(k, 1) + 2 * bit(k, 3), bit(k, 4), bit(k, 0) + 2 * bit(k, 2)


def exchange_kernel(
    field_ref, signs_ref, nbrs_ref, mu_ref, eps_ref, owner_ref, map_ref, stiffness_ref, mass_ref,
    squares_ref, received_ref, both_ref,
    oriented, traces, halo_traces, halo_nbrs, signs, nbrs, mu, eps, owner, tmap, scale, high_ref, low_ref, payload, bundle,
    reply_out, reply_in, own_parts, halo_parts, columns, picks_ref, matrices, both,
    in_sem, halo_send, halo_recv, a_send, a_recv, f_send, f_recv, own_sem, reply_send, reply_recv, both_sem,
):
    gx = lax.axis_index("gx")
    yz = lax.axis_index("yz")
    gx_size = lax.axis_size("gx")
    yz_size = lax.axis_size("yz")
    devices = gx_size * yz_size
    me = gx * yz_size + yz
    z, c = lax.div(gx, 2), lax.rem(gx, 2)
    y, x = lax.div(yz, 4), lax.rem(yz, 4)
    plane = gx * 4 + y
    planes = devices // 4
    dofs, count = oriented.shape
    depth = payload.shape[1]
    block = count // CHUNKS

    def at(index):
        return (lax.div(index, yz_size), lax.rem(index, yz_size))

    def in_plane(p):
        return (lax.div(p, 4), lax.rem(p, 4) * 4 + x)

    def target(k):
        oz, oc, oy = offsets(k)
        return (lax.rem(z + oz, 4) * 2 + lax.rem(c + oc, 2)) * 4 + lax.rem(y + oy, 4)

    def source(k):
        oz, oc, oy = offsets(k)
        return (lax.rem(z + 4 - oz, 4) * 2 + lax.rem(c + 2 - oc, 2)) * 4 + lax.rem(y + 4 - oy, 4)

    following = lax.rem(me + 1, devices)
    preceding = lax.rem(me + devices - 1, devices)
    ahead, behind = at(following), at(preceding)
    up_index = jnp.where(c == 0, preceding, following)
    down_index = jnp.where(c == 0, following, preceding)
    up, down = at(up_index), at(down_index)
    sink = (c == 1) & (yz == 0)
    source_end = (c == 0) & (yz == 0)
    halo_count = jnp.where(sink, 2, jnp.where(source_end, 0, 1))
    landing_slot = jnp.where((c == 0) & (yz == yz_size - 1), 1, 0)
    reply_slot = jnp.where((c == 1) & (yz == yz_size - 1), 1, 0)

    loads = [
        pltpu.make_async_copy(signs_ref, signs, in_sem.at[0]),
        pltpu.make_async_copy(map_ref, tmap, in_sem.at[1]),
    ]
    fields = []
    for part in range(CHUNKS):
        cols = pl.ds(part * block, block)
        fields.append(pltpu.make_async_copy(field_ref.at[:, cols], oriented.at[:, cols], in_sem.at[2 + part]))
    later = [
        pltpu.make_async_copy(s, d, in_sem.at[2 + CHUNKS + i])
        for i, (s, d) in enumerate(
            (
                (owner_ref, owner), (mu_ref, mu), (eps_ref, eps), (nbrs_ref, nbrs),
                (stiffness_ref, matrices.at[0]), (mass_ref, matrices.at[1]),
            )
        )
    ]
    for copy in loads + fields + later:
        copy.start()

    barrier = pltpu.get_barrier_semaphore()

    def greet(k, carry):
        pl.semaphore_signal(barrier, inc=1, device_id=in_plane(target(k)), device_id_type=MESH)
        return carry

    lax.fori_loop(1, planes, greet, 0)
    for step in range(1, 4):
        pl.semaphore_signal(barrier, inc=1, device_id=(gx, y * 4 + lax.rem(x + step, 4)), device_id_type=MESH)
    pl.semaphore_signal(barrier, inc=1, device_id=ahead, device_id_type=MESH)
    pl.semaphore_signal(barrier, inc=1, device_id=behind, device_id_type=MESH)

    edges = signs.shape[0]
    rows = lax.broadcasted_iota(jnp.int32, (40, edges), 0)
    edge = lax.broadcasted_iota(jnp.int32, (40, edges), 1)
    picks = ((rows < 36) & (rows % 3 != 1) & (rows // 3 == edge)).astype(jnp.bfloat16)

    def halo_copy(part, lane_of, slot, peer):
        cols = pl.ds(part * block, block)
        if part == CHUNKS:
            src, dst = nbrs, halo_nbrs.at[slot]
        else:
            src, dst = traces.at[:, cols], halo_traces.at[slot, :, cols]
        return pltpu.make_async_remote_copy(
            src_ref=src, dst_ref=dst, send_sem=halo_send.at[lane_of, part], recv_sem=halo_recv.at[slot, part],
            device_id=peer, device_id_type=MESH,
        )

    def halo_start(part):
        @pl.when(jnp.logical_not(sink))
        def _():
            halo_copy(part, 0, landing_slot, down).start()

        @pl.when(source_end)
        def _():
            halo_copy(part, 1, 0, up).start()

    for copy in loads:
        copy.wait()
    map_parts = stacked_left(tmap[...])
    for part in range(CHUNKS):
        cols = slice(part * block, (part + 1) * block)
        fields[part].wait()
        shifted = (signs[:, cols] - 1).astype(jnp.float32).astype(jnp.bfloat16)
        factor = 1.0 + jnp.dot(picks, shifted, preferred_element_type=jnp.float32)
        oriented[0:40, cols] = oriented[0:40, cols] * factor
        traces[:, cols] = stacked_product(map_parts, oriented[:, cols])
        if part == 1:
            pl.semaphore_wait(barrier, planes - 1 + 3 + 2)
        if part >= 1:
            halo_start(part - 1)
    for copy in later:
        copy.wait()
    halo_start(CHUNKS)

    tiles = count // LANES
    bf = jnp.bfloat16
    sub = lax.broadcasted_iota(jnp.int32, (LANES, LANES), 0)
    lane_full = lax.broadcasted_iota(jnp.int32, (LANES, LANES), 1)
    upto = (sub <= lane_full).astype(jnp.float32).astype(bf)
    ones = jnp.ones((LANES, LANES), bf)
    before = jnp.zeros((LANES, LANES), jnp.float32)
    nt = (((1,), (1,)), ((), ()))
    table = jnp.zeros((3 * planes, LANES), jnp.float32)
    sub8 = lax.broadcasted_iota(jnp.int32, (8, LANES), 0)
    for tile in range(tiles):
        cols = slice(tile * LANES, (tile + 1) * LANES)
        scale[:, cols] = jnp.where(sub8 == 0, row8(mu[:, cols]), jnp.where(sub8 == 1, row8(eps[:, cols]), 0.0))
        own = owner[:, cols]
        onehot = sub == own
        hot = onehot.astype(jnp.float32)
        hot16 = hot.astype(bf)
        ordinal = before + jnp.dot(hot16, upto, preferred_element_type=jnp.float32) - 1.0
        rank = jnp.sum(jnp.where(onehot, ordinal, 0.0), axis=0, keepdims=True)
        before = before + jnp.dot(hot16, ones, preferred_element_type=jnp.float32)
        place = (own & 3) * 32 + rank.astype(jnp.int32)
        landing = (sub == place).astype(jnp.float32).astype(bf)
        group = lax.broadcasted_iota(jnp.int32, (planes, LANES), 0) == (own >> 2)
        groupf = group.astype(jnp.float32)
        lane_row = lax.broadcasted_iota(jnp.int32, (planes, LANES), 1).astype(jnp.float32)
        parts = jnp.concatenate([groupf, groupf * lane_row, groupf * float(tile)], axis=0).astype(bf)
        table = table + lax.dot_general(parts, landing, nt, preferred_element_type=jnp.float32)
    found = table[:planes]
    high_ref[...] = jnp.where(found > 0.5, table[2 * planes :], -1.0).astype(jnp.int32)
    low_ref[...] = table[planes : 2 * planes].astype(jnp.int32)
    halo_start(CHUNKS - 1)

    lane = lax.broadcasted_iota(jnp.int32, (8, LANES), 1)
    pair = 2 * LANES
    sub_pair = lax.broadcasted_iota(jnp.int32, (LANES, pair), 0)
    height = 4 * depth
    for part in range(CHUNKS):
        cols = slice(part * block, (part + 1) * block)
        filler = jnp.zeros((height - dofs - 8, block), jnp.float32)
        value = jnp.concatenate([oriented[:, cols], scale[:, cols], filler], axis=0)
        columns[0:height, cols], columns[height:, cols] = split3(value)

    def pack_pair(k):
        two = (target(k), target(k + 1))
        high = jnp.concatenate([high_ref[pl.ds(t, 1), :] for t in two], axis=1)
        low = jnp.concatenate([low_ref[pl.ds(t, 1), :] for t in two], axis=1)
        pick = (sub_pair == low).astype(jnp.float32).astype(bf)
        for tile in range(tiles):
            gate = jnp.broadcast_to((high == tile).astype(jnp.float32), (16, pair)).astype(bf)
            picks_ref[tile * LANES : (tile + 1) * LANES, :] = pick * jnp.concatenate([gate] * 8, axis=0)
        found = jnp.dot(columns[...], picks_ref[...], preferred_element_type=jnp.float32)
        value = found[:height] + found[height:]
        for h, t in enumerate(two):
            lanes = slice(h * LANES, (h + 1) * LANES)
            for i in range(depth // 8):
                outs = quarter_swap([value[32 * i + 8 * q : 32 * i + 8 * q + 8, lanes] for q in range(4)], lane)
                for q in range(4):
                    payload[4 * t + q, 8 * i : 8 * i + 8, :] = outs[q]

    def send_group(k):
        t = target(k)
        pltpu.make_async_remote_copy(
            src_ref=payload.at[pl.ds(4 * t, 4)], dst_ref=bundle.at[pl.ds(4 * plane, 4)], send_sem=a_send,
            recv_sem=a_recv.at[plane], device_id=in_plane(t), device_id_type=MESH,
        ).start()

    def forward(origin, s):
        for step in range(1, 4):
            xd = lax.rem(x + step, 4)
            pltpu.make_async_remote_copy(
                src_ref=origin.at[4 * s + xd], dst_ref=received_ref.at[4 * s + x], send_sem=f_send, recv_sem=f_recv,
                device_id=(gx, y * 4 + xd), device_id_type=MESH,
            ).start()
        pltpu.make_async_copy(origin.at[4 * s + x], received_ref.at[4 * s + x], own_sem).start()

    def forward_step(k):
        s = source(k)
        pltpu.make_async_remote_copy(
            src_ref=payload.at[pl.ds(4 * s, 4)], dst_ref=bundle.at[pl.ds(4 * s, 4)], send_sem=a_send,
            recv_sem=a_recv.at[s], device_id=ahead, device_id_type=MESH,
        ).wait_recv()
        forward(bundle, s)

    lag = 6

    def pack_step(m, carry):
        pack_pair(2 * m)

        @pl.when(m == 1)
        def _():
            forward(payload, plane)

        @pl.when(m > 1)
        def _():
            send_group(2 * m - 2)

        @pl.when(m > 0)
        def _():
            send_group(2 * m - 1)

        @pl.when(m >= lag)
        def _():
            forward_step(m - lag + 1)

        return carry

    lax.fori_loop(0, planes // 2, pack_step, 0)
    send_group(planes - 2)
    send_group(planes - 1)
    done = planes // 2 - lag + 1

    width = dofs // 6
    vecs = width // 8

    def split_table(table, out):
        for o, odd in enumerate(MATRIX_FACES):
            rows_o = slice(odd * width, (odd + 1) * width)
            for tile in range(0, tiles, 2):
                stacked = jnp.concatenate(
                    [table[rows_o, (tile + i) * LANES : (tile + i + 1) * LANES] for i in range(2)], axis=0
                )
                high, low = split3(stacked)
                out[o, tile * width : (tile + 2) * width, 0:LANES] = high
                out[o, tile * width : (tile + 2) * width, LANES:] = low

    def jump_tile(step, faces, face_nbrs, table, parts, base, alone):
        cols = pl.ds(pl.multiple_of(step * pair, pair), pair)
        total = jnp.zeros((8, pair), jnp.float32)
        for face in range(6):
            other = face ^ 1
            nbr = jnp.broadcast_to(face_nbrs[face : face + 1, cols], (8, pair))
            spot = nbr - base
            high = spot >> 7
            low = spot & (LANES - 1)
            if other in MATRIX_FACES:
                pick = (sub_pair == low[0:1]).astype(jnp.float32).astype(jnp.bfloat16)
                found = jnp.dot(
                    parts[MATRIX_FACES.index(other)], jnp.concatenate([pick, pick], axis=0), preferred_element_type=jnp.float32
                )
                got = [jnp.zeros((8, pair), jnp.float32) for _ in range(vecs)]
                for tile in range(tiles):
                    hit = high == tile
                    for v in range(vecs):
                        r = tile * width + 8 * v
                        got[v] = jnp.where(hit, found[r : r + 8], got[v])
            else:
                halves = []
                for h in range(2):
                    lanes = slice(h * LANES, (h + 1) * LANES)
                    half = [jnp.zeros((8, LANES), jnp.float32) for _ in range(vecs)]
                    for tile in range(tiles):
                        hit = high[:, lanes] == tile
                        for v in range(vecs):
                            r = other * width + 8 * v
                            piece = table[r : r + 8, tile * LANES : (tile + 1) * LANES]
                            half[v] = jnp.where(hit, lane_gather(piece, low[:, lanes]), half[v])
                    halves.append(half)
                got = [jnp.concatenate([halves[0][v], halves[1][v]], axis=1) for v in range(vecs)]
            here = (spot >= 0) & (spot < count)
            if alone:
                here = here | (nbr < 0)
            for v in range(vecs):
                r = face * width + 8 * v
                jump = faces[r : r + 8, cols] - got[v]
                total = total + jnp.where(here, jump * jump, 0.0)
        return cols, jnp.sum(total, axis=0, keepdims=True)

    own_base = me * count

    for i in range(2):
        both[dofs * i : dofs * (i + 1)] = stacked_left(matrices[i])
    hand_over = pltpu.make_async_copy(both, both_ref, both_sem)
    split_table(traces, own_parts)

    hand_over.start()

    def own_step(step, carry):
        forward_step(done + step)
        cols, row = jump_tile(step, traces, nbrs, traces, own_parts, own_base, True)
        squares_ref[:, cols] = row
        return carry

    lax.fori_loop(0, tiles // 2, own_step, 0)
    rest = done + tiles // 2

    def halo_step(i, carry):
        for part in range(CHUNKS + 1):
            halo_copy(part, 0, i, up).wait_recv()
        base = jnp.where(i == 0, up_index, down_index) * count
        split_table(halo_traces.at[i], halo_parts)

        def across(step, inner):
            first = rest + jnp.where(sink, i * (tiles // 2) + step, 2 * step)
            second = rest + 2 * step + 1

            @pl.when(first < planes)
            def _():
                forward_step(first)

            @pl.when(jnp.logical_not(sink) & (second < planes))
            def _():
                forward_step(second)

            cols, row = jump_tile(step, traces, nbrs, halo_traces.at[i], halo_parts, base, False)
            squares_ref[:, cols] = squares_ref[:, cols] + row
            cols, row = jump_tile(step, halo_traces.at[i], halo_nbrs.at[i], traces, own_parts, own_base, False)
            reply_out[i, :, cols] = row
            return inner

        lax.fori_loop(0, tiles // 2, across, 0)
        return carry

    lax.fori_loop(0, halo_count, halo_step, 0)

    @pl.when(source_end)
    def _():
        def remaining(k, carry):
            forward_step(k)
            return carry

        lax.fori_loop(rest, planes, remaining, 0)

    def reply(slot, landing, peer):
        return pltpu.make_async_remote_copy(
            src_ref=reply_out.at[slot], dst_ref=reply_in.at[landing], send_sem=reply_send.at[slot],
            recv_sem=reply_recv.at[landing], device_id=peer, device_id_type=MESH,
        )

    @pl.when(jnp.logical_not(source_end))
    def _():
        reply(0, reply_slot, up).start()

    @pl.when(sink)
    def _():
        reply(1, 0, down).start()

    @pl.when(jnp.logical_not(sink))
    def _():
        reply(0, 0, up).wait_recv()
        squares_ref[...] = squares_ref[...] + reply_in[0]

    @pl.when(source_end)
    def _():
        reply(0, 1, up).wait_recv()
        squares_ref[...] = squares_ref[...] + reply_in[1]

    hand_over.wait()
    @pl.when(jnp.logical_not(source_end))
    def _():
        reply(0, reply_slot, up).wait_send()

    @pl.when(sink)
    def _():
        reply(1, 0, down).wait_send()

    for part in range(CHUNKS + 1):

        @pl.when(jnp.logical_not(sink))
        def _():
            halo_copy(part, 0, landing_slot, down).wait_send()

        @pl.when(source_end)
        def _():
            halo_copy(part, 1, 0, up).wait_send()

    sent = 4 * (planes - 1)
    pltpu.make_async_remote_copy(
        src_ref=payload.at[pl.ds(0, sent)], dst_ref=bundle.at[pl.ds(0, sent)], send_sem=a_send, recv_sem=a_recv.at[0],
        device_id=ahead, device_id_type=MESH,
    ).wait_send()
    moved = 3 * planes
    along = pltpu.make_async_remote_copy(
        src_ref=bundle.at[pl.ds(0, moved)], dst_ref=received_ref.at[pl.ds(0, moved)], send_sem=f_send, recv_sem=f_recv,
        device_id=ahead, device_id_type=MESH,
    )
    along.wait_send()
    along.wait_recv()
    pltpu.make_async_copy(bundle.at[pl.ds(0, planes)], received_ref.at[pl.ds(0, planes)], own_sem).wait()


def exchange(field, edge_signs, face_nbrs, mu, eps, owner, trace_map, stiffness, mass, devices):
    dofs, count = field.shape
    planes = devices // 4
    depth = 8 * ((dofs // 8 + 1 + 3) // 4)
    anywhere = pl.BlockSpec(memory_space=pl.ANY)
    wide = pltpu.VMEM((dofs, count), jnp.float32)
    blocks = pltpu.VMEM((devices, depth, LANES), jnp.float32)
    row = pltpu.VMEM((1, count), jnp.float32)
    parts = pltpu.VMEM((len(MATRIX_FACES), count // LANES * dofs // 6, 2 * LANES), jnp.bfloat16)
    dma = pltpu.SemaphoreType.DMA
    return pl.pallas_call(
        exchange_kernel,
        in_specs=[anywhere] * 9,
        out_specs=[pl.BlockSpec(memory_space=pltpu.VMEM), anywhere, anywhere],
        out_shape=[
            jax.ShapeDtypeStruct((1, count), jnp.float32),
            jax.ShapeDtypeStruct((devices, depth, LANES), jnp.float32),
            jax.ShapeDtypeStruct((2 * dofs, 3 * dofs), jnp.bfloat16),
        ],
        scratch_shapes=[
            wide, wide, pltpu.VMEM((2, dofs, count), jnp.float32), pltpu.VMEM((2, *face_nbrs.shape), jnp.int32),
            pltpu.VMEM(edge_signs.shape, jnp.int32),
            pltpu.VMEM(face_nbrs.shape, jnp.int32),
            row, row, pltpu.VMEM((1, count), jnp.int32),
            pltpu.VMEM(trace_map.shape, jnp.float32),
            pltpu.VMEM((8, count), jnp.float32),
            pltpu.VMEM((planes, LANES), jnp.int32),
            pltpu.VMEM((planes, LANES), jnp.int32),
            blocks, blocks,
            pltpu.VMEM((2, 1, count), jnp.float32), pltpu.VMEM((2, 1, count), jnp.float32), parts, parts,
            pltpu.VMEM((8 * depth, count), jnp.bfloat16), pltpu.VMEM((count, 2 * LANES), jnp.bfloat16),
            pltpu.VMEM((2, dofs, dofs), jnp.float32), pltpu.VMEM((2 * dofs, 3 * dofs), jnp.bfloat16),
            dma((CHUNKS + 8,)), dma((2, CHUNKS + 1)), dma((2, CHUNKS + 1)), dma, dma((planes,)), dma, dma, dma,
            dma((2,)), dma((2,)), dma,
        ],
        compiler_params=pltpu.CompilerParams(collective_id=0, has_side_effects=True, vmem_limit_bytes=VMEM_LIMIT),
        name="exchange",
    )(field, edge_signs, face_nbrs, mu, eps, owner, trace_map, stiffness, mass)


def apply_kernel(
    received_ref, both_ref, squares_ref, size_ref, migrated_ref, applied_ref, out_ref
):
    @pl.when(pl.program_id(0) == 0)
    def _():
        out_ref[...] = jnp.sqrt(size_ref[...] * (squares_ref[...] / migrated_ref.shape[0]) + 1e-06)

    lane = lax.broadcasted_iota(jnp.int32, (8, LANES), 1)
    dofs = migrated_ref.shape[0]
    rows = dofs // 8
    both = both_ref[...]
    for t in range(0, received_ref.shape[0] // 4, 2):
        cols = slice(t * LANES, (t + 2) * LANES)
        found = [[], []]
        for h in range(2):
            for i in range(received_ref.shape[1] // 8):
                block = [received_ref[4 * (t + h) + q, 8 * i : 8 * i + 8, :] for q in range(4)]
                found[h].extend(quarter_swap(block, lane))
        value = jnp.concatenate([jnp.concatenate(part[:rows], axis=0) for part in found], axis=1)
        scale = jnp.concatenate([part[rows] for part in found], axis=1)
        migrated_ref[:, cols] = value
        product = stacked_product(both, value)
        applied_ref[:, cols] = scale[0:1] * product[:dofs] + scale[1:2] * product[dofs:]


def apply_received(received, both, squares, size):
    devices, depth, _ = received.shape
    dofs = both.shape[0] // 2
    per = 32
    block = per * 32
    return pl.pallas_call(
        apply_kernel,
        grid=(devices // per,),
        in_specs=[
            pl.BlockSpec((per, depth, LANES), lambda i: (i, 0, 0)),
            pl.BlockSpec(both.shape, lambda i: (0, 0)),
            pl.BlockSpec(squares.shape, lambda i: (0, 0)),
            pl.BlockSpec(squares.shape, lambda i: (0, 0)),
        ],
        out_specs=[pl.BlockSpec((dofs, block), lambda i: (0, i))] * 2 + [pl.BlockSpec(squares.shape, lambda i: (0, 0))],
        out_shape=[jax.ShapeDtypeStruct((dofs, devices * 32), jnp.float32)] * 2
        + [jax.ShapeDtypeStruct(squares.shape, jnp.float32)],
        compiler_params=pltpu.CompilerParams(vmem_limit_bytes=VMEM_LIMIT),
        cost_estimate=pl.CostEstimate(flops=10**9, bytes_accessed=8 * 10**6, transcendentals=0),
        name="apply",
    )(received, both, squares, size)


def body(field, edge_signs, face_nbrs, elem_size, mu_inv, permittivity, new_owner, trace_map, stiffness, mass):
    count = field.shape[1]
    devices = lax.axis_size(AXES)
    row = (1, count)
    squares, received, both = exchange(
        field, edge_signs, face_nbrs, mu_inv.reshape(row), permittivity.reshape(row), new_owner.reshape(row),
        trace_map, stiffness, mass, devices,
    )
    migrated, applied, indicators = apply_received(received, both, squares, elem_size.reshape(row))
    return indicators.reshape(count), migrated, applied


def solution(mesh):
    flat = P(AXES)
    wide = P(None, AXES)
    in_specs = (wide, wide, wide, flat, flat, flat, P(AXES, None), P(), P(), P())
    return jax.shard_map(body, mesh=mesh, in_specs=in_specs, out_specs=(flat, wide, wide), check_vma=False)
```

time: 83 us -> 71.6 us (0.86); the launches traced: 81.5 us -> 71.4 us
  Pallas kernels: 80.9 us -> 70.8 us
    pallas_call x1, Pallas kernels: 72.6 us -> 65.3 us  [exchange(): pl.pallas_call(exchange_kernel, in_specs=[anywhere] * 9, out_specs=[pl.Bl...]
    pallas_call x1, Pallas kernels: 8.24 us -> 5.48 us  [apply_received(): pl.pallas_call(apply_kernel, grid=(devices // per,), in_specs=[pl.BlockSp...]
where the time goes in v3:
time: 71.6 us; the launch traced here: 71.4 us
  Pallas kernels  70.8 us (99%)
    pallas_call x1, Pallas kernels, exchange(): pl.pallas_call(exchange_kernel, in_specs=[anywhere] * 9, out_specs=[pl.Bl...  65.3 us
    pallas_call x1, Pallas kernels, apply_received(): pl.pallas_call(apply_kernel, grid=(devices // per,), in_specs=[pl.BlockSp...  5.48 us

profile of v3, /device:TPU:26, one launch (start us, length us, event | category | flops | bytes accessed | tf_op | source)
XLA Modules:
  0.0 71.4 jit_solution(17959020366768813533)
XLA Ops:
  0.6 65.3 %exchange.1 = (f32[1,2048]{1,0:T(1,128)}, f32[128,40,128]{2,1,0:T(8,128)}, bf16[288,432]{1,0:T(8,128)(2,1)}) custom-call(f32[144,2048]{1,0:T(8,128)} %field_ref.1, s32[12,2048]{1,0:T(8,128)} %signs_ref.1, s32[6,2048]{1,0:T(8,128)} %nbrs_ref.1, f32[1,2048]{1,0:T(1,128)} %bitcast.5, f32[1,2048]{1,0:T(1,128)} %bitcast.6, s32[1,2048]{1,0:T(1,128)} %bitcast.7, ...), custom_call_target="tpu_custom_call" | custom-call | tf_op jit(solution)/shard_map/exchange/pallas_call | solution.py:479
  65.9 5.5 %apply.1 = (f32[144,4096]{1,0:T(8,128)}, f32[144,4096]{1,0:T(8,128)}, f32[1,2048]{1,0:T(1,128)}) custom-call(f32[128,40,128]{2,1,0:T(8,128)} %get-tuple-element.9.received_ref, bf16[288,432]{1,0:T(8,128)(2,1)} %get-tuple-element.10.both_ref, f32[1,2048]{1,0:T(1,128)} %get-tuple-element.11.squares_ref, f32[1,2048]{1,0:T(1,128)} %bitcast.8), custom_call_target="tpu_custom_call" | custom-call | flops 1000000000 | bytes 8000000 | tf_op jit(solution)/shard_map/apply/pallas_call | solution.py:539

commit v4 on v3

--- a/solution.py
+++ b/solution.py
@@ -221,12 +221,21 @@
     lane = lax.broadcasted_iota(jnp.int32, (8, LANES), 1)
     pair = 2 * LANES
     sub_pair = lax.broadcasted_iota(jnp.int32, (LANES, pair), 0)
-    height = 4 * depth
+    groups = -(-depth // 8)
+    tail = depth - 8 * (groups - 1)
+    height = 32 * groups
+    main = 32 * (groups - 1)
+    spot_row = lax.broadcasted_iota(jnp.int32, (32, dofs - main + 8), 0)
+    item = lax.broadcasted_iota(jnp.int32, (32, dofs - main + 8), 1)
+    inner = lax.rem(spot_row, 8)
+    places = ((inner < tail) & (item == lax.div(spot_row, 8) * tail + inner)).astype(jnp.float32).astype(bf)
     for part in range(CHUNKS):
         cols = slice(part * block, (part + 1) * block)
-        filler = jnp.zeros((height - dofs - 8, block), jnp.float32)
-        value = jnp.concatenate([oriented[:, cols], scale[:, cols], filler], axis=0)
-        columns[0:height, cols], columns[height:, cols] = split3(value)
+        columns[0:main, cols], columns[height : height + main, cols] = split3(oriented[0:main, cols])
+        rest_parts = split3(jnp.concatenate([oriented[main:, cols], scale[:, cols]], axis=0))
+        for i, piece in enumerate(rest_parts):
+            moved_rows = jnp.dot(places, piece, preferred_element_type=jnp.float32).astype(bf)
+            columns[height * i + main : height * (i + 1), cols] = moved_rows
 
     def pack_pair(k):
         two = (target(k), target(k + 1))
@@ -240,10 +249,11 @@
         value = found[:height] + found[height:]
         for h, t in enumerate(two):
             lanes = slice(h * LANES, (h + 1) * LANES)
-            for i in range(depth // 8):
+            for i in range(groups):
                 outs = quarter_swap([value[32 * i + 8 * q : 32 * i + 8 * q + 8, lanes] for q in range(4)], lane)
+                kept = 8 if i < groups - 1 else tail
                 for q in range(4):
-                    payload[4 * t + q, 8 * i : 8 * i + 8, :] = outs[q]
+                    payload[4 * t + q, 8 * i : 8 * i + kept, :] = outs[q][:kept]
 
     def send_group(k):
         t = target(k)
@@ -469,7 +479,7 @@
 def exchange(field, edge_signs, face_nbrs, mu, eps, owner, trace_map, stiffness, mass, devices):
     dofs, count = field.shape
     planes = devices // 4
-    depth = 8 * ((dofs // 8 + 1 + 3) // 4)
+    depth = -(-(dofs + 2) // 4)
     anywhere = pl.BlockSpec(memory_space=pl.ANY)
     wide = pltpu.VMEM((dofs, count), jnp.float32)
     blocks = pltpu.VMEM((devices, depth, LANES), jnp.float32)
@@ -496,7 +506,7 @@
             pltpu.VMEM((planes, LANES), jnp.int32),
             blocks, blocks,
             pltpu.VMEM((2, 1, count), jnp.float32), pltpu.VMEM((2, 1, count), jnp.float32), parts, parts,
-            pltpu.VMEM((8 * depth, count), jnp.bfloat16), pltpu.VMEM((count, 2 * LANES), jnp.bfloat16),
+            pltpu.VMEM((64 * -(-depth // 8), count), jnp.bfloat16), pltpu.VMEM((count, 2 * LANES), jnp.bfloat16),
             pltpu.VMEM((2, dofs, dofs), jnp.float32), pltpu.VMEM((2 * dofs, 3 * dofs), jnp.bfloat16),
             dma((CHUNKS + 8,)), dma((2, CHUNKS + 1)), dma((2, CHUNKS + 1)), dma, dma((planes,)), dma, dma, dma,
             dma((2,)), dma((2,)), dma,
@@ -515,17 +525,22 @@
 
     lane = lax.broadcasted_iota(jnp.int32, (8, LANES), 1)
     dofs = migrated_ref.shape[0]
-    rows = dofs // 8
+    groups = -(-received_ref.shape[1] // 8)
+    tail = received_ref.shape[1] - 8 * (groups - 1)
     both = both_ref[...]
     for t in range(0, received_ref.shape[0] // 4, 2):
         cols = slice(t * LANES, (t + 2) * LANES)
         found = [[], []]
         for h in range(2):
-            for i in range(received_ref.shape[1] // 8):
-                block = [received_ref[4 * (t + h) + q, 8 * i : 8 * i + 8, :] for q in range(4)]
-                found[h].extend(quarter_swap(block, lane))
-        value = jnp.concatenate([jnp.concatenate(part[:rows], axis=0) for part in found], axis=1)
-        scale = jnp.concatenate([part[rows] for part in found], axis=1)
+            for i in range(groups):
+                kept = 8 if i < groups - 1 else tail
+                block = [received_ref[4 * (t + h) + q, 8 * i : 8 * i + kept, :] for q in range(4)]
+                if kept < 8:
+                    block = [jnp.concatenate([b, jnp.zeros((8 - kept, LANES), jnp.float32)], axis=0) for b in block]
+                found[h].extend(piece[:kept] for piece in quarter_swap(block, lane))
+        stacked = [jnp.concatenate(part, axis=0) for part in found]
+        value = jnp.concatenate([part[:dofs] for part in stacked], axis=1)
+        scale = jnp.concatenate([part[dofs : dofs + 2] for part in stacked], axis=1)
         migrated_ref[:, cols] = value
         product = stacked_product(both, value)
         applied_ref[:, cols] = scale[0:1] * product[:dofs] + scale[1:2] * product[dofs:]

time: 71.6 us -> 70.1 us (0.979); the launches traced: 71.4 us -> 68.7 us
  Pallas kernels: 70.8 us -> 68 us
    pallas_call x1, Pallas kernels: 65.3 us -> 62.4 us  [exchange(): pl.pallas_call(exchange_kernel, in_specs=[anywhere] * 9, out_specs=[pl.Bl...]
where the time goes in v4:
time: 70.1 us; the launch traced here: 68.7 us
  Pallas kernels  68 us (97%)
    pallas_call x1, Pallas kernels, exchange(): pl.pallas_call(exchange_kernel, in_specs=[anywhere] * 9, out_specs=[pl.Bl...  62.4 us
    pallas_call x1, Pallas kernels, apply_received(): pl.pallas_call(apply_kernel, grid=(devices // per,), in_specs=[pl.BlockSp...  5.66 us

profile of v4, /device:TPU:26, one launch (start us, length us, event | category | flops | bytes accessed | tf_op | source)
XLA Modules:
  0.0 68.7 jit_solution(1900885618959187925)
XLA Ops:
  0.6 62.4 %exchange.1 = (f32[1,2048]{1,0:T(1,128)}, f32[128,37,128]{2,1,0:T(8,128)}, bf16[288,432]{1,0:T(8,128)(2,1)}) custom-call(f32[144,2048]{1,0:T(8,128)} %field_ref.1, s32[12,2048]{1,0:T(8,128)} %signs_ref.1, s32[6,2048]{1,0:T(8,128)} %nbrs_ref.1, f32[1,2048]{1,0:T(1,128)} %bitcast.5, f32[1,2048]{1,0:T(1,128)} %bitcast.6, s32[1,2048]{1,0:T(1,128)} %bitcast.7, ...), custom_call_target="tpu_custom_call" | custom-call | tf_op jit(solution)/shard_map/exchange/pallas_call | solution.py:489
  63.0 5.7 %apply.1 = (f32[144,4096]{1,0:T(8,128)}, f32[144,4096]{1,0:T(8,128)}, f32[1,2048]{1,0:T(1,128)}) custom-call(f32[128,37,128]{2,1,0:T(8,128)} %get-tuple-element.9.received_ref, bf16[288,432]{1,0:T(8,128)(2,1)} %get-tuple-element.10.both_ref, f32[1,2048]{1,0:T(1,128)} %get-tuple-element.11.squares_ref, f32[1,2048]{1,0:T(1,128)} %bitcast.8), custom_call_target="tpu_custom_call" | custom-call | flops 1000000000 | bytes 8000000 | tf_op jit(solution)/shard_map/apply/pallas_call | solution.py:554

commit v5 on v4

--- a/solution.py
+++ b/solution.py
@@ -61,7 +61,7 @@
 
 
 def offsets(k):
-    return bit(k, 1) + 2 * bit(k, 3), bit(k, 4), bit(k, 0) + 2 * bit(k, 2)
+    return bit(k, 2) + 2 * bit(k, 3), bit(k, 4), bit(k, 0) + 2 * bit(k, 1)
 
 
 def exchange_kernel(
@@ -279,7 +279,7 @@
         ).wait_recv()
         forward(bundle, s)
 
-    lag = 6
+    lag = 8
 
     def pack_step(m, carry):
         pack_pair(2 * m)
@@ -549,7 +549,7 @@
 def apply_received(received, both, squares, size):
     devices, depth, _ = received.shape
     dofs = both.shape[0] // 2
-    per = 32
+    per = 64
     block = per * 32
     return pl.pallas_call(
         apply_kernel,

time: 70.1 us -> 67.7 us (0.966); the launches traced: 68.7 us -> 67.4 us
  Pallas kernels: 68 us -> 66.7 us
    pallas_call x1, Pallas kernels: 5.66 us -> 4.85 us  [apply_received(): pl.pallas_call(apply_kernel, grid=(devices // per,), in_specs=[pl.BlockSp...]
where the time goes in v5:
time: 67.7 us; the launch traced here: 67.4 us
  Pallas kernels  66.7 us (99%)
    pallas_call x1, Pallas kernels, exchange(): pl.pallas_call(exchange_kernel, in_specs=[anywhere] * 9, out_specs=[pl.Bl...  61.9 us
    pallas_call x1, Pallas kernels, apply_received(): pl.pallas_call(apply_kernel, grid=(devices // per,), in_specs=[pl.BlockSp...  4.85 us

profile of v5, /device:TPU:26, one launch (start us, length us, event | category | flops | bytes accessed | tf_op | source)
XLA Modules:
  0.0 67.4 jit_solution(13857706345831364948)
XLA Ops:
  0.6 61.9 %exchange.1 = (f32[1,2048]{1,0:T(1,128)}, f32[128,37,128]{2,1,0:T(8,128)}, bf16[288,432]{1,0:T(8,128)(2,1)}) custom-call(f32[144,2048]{1,0:T(8,128)} %field_ref.1, s32[12,2048]{1,0:T(8,128)} %signs_ref.1, s32[6,2048]{1,0:T(8,128)} %nbrs_ref.1, f32[1,2048]{1,0:T(1,128)} %bitcast.5, f32[1,2048]{1,0:T(1,128)} %bitcast.6, s32[1,2048]{1,0:T(1,128)} %bitcast.7, ...), custom_call_target="tpu_custom_call" | custom-call | tf_op jit(solution)/shard_map/exchange/pallas_call | solution.py:489
  62.5 4.9 %apply.1 = (f32[144,4096]{1,0:T(8,128)}, f32[144,4096]{1,0:T(8,128)}, f32[1,2048]{1,0:T(1,128)}) custom-call(f32[128,37,128]{2,1,0:T(8,128)} %get-tuple-element.9.received_ref, bf16[288,432]{1,0:T(8,128)(2,1)} %get-tuple-element.10.both_ref, f32[1,2048]{1,0:T(1,128)} %get-tuple-element.11.squares_ref, f32[1,2048]{1,0:T(1,128)} %bitcast.8), custom_call_target="tpu_custom_call" | custom-call | flops 1000000000 | bytes 8000000 | tf_op jit(solution)/shard_map/apply/pallas_call | solution.py:554

commit v6 on v5

--- a/solution.py
+++ b/solution.py
@@ -279,7 +279,7 @@
         ).wait_recv()
         forward(bundle, s)
 
-    lag = 8
+    lag = 9
 
     def pack_step(m, carry):
         pack_pair(2 * m)

time: 67.7 us -> 67.8 us (level)
  no operation moved by 1% of the time
where the time goes in v6:
time: 67.8 us; the launch traced here: 67.4 us
  Pallas kernels  66.7 us (98%)
    pallas_call x1, Pallas kernels, exchange(): pl.pallas_call(exchange_kernel, in_specs=[anywhere] * 9, out_specs=[pl.Bl...  61.9 us
    pallas_call x1, Pallas kernels, apply_received(): pl.pallas_call(apply_kernel, grid=(devices // per,), in_specs=[pl.BlockSp...  4.85 us

profile of v6, /device:TPU:26, one launch (start us, length us, event | category | flops | bytes accessed | tf_op | source)
XLA Modules:
  0.0 67.4 jit_solution(7149752754167424465)
XLA Ops:
  0.6 61.9 %exchange.1 = (f32[1,2048]{1,0:T(1,128)}, f32[128,37,128]{2,1,0:T(8,128)}, bf16[288,432]{1,0:T(8,128)(2,1)}) custom-call(f32[144,2048]{1,0:T(8,128)} %field_ref.1, s32[12,2048]{1,0:T(8,128)} %signs_ref.1, s32[6,2048]{1,0:T(8,128)} %nbrs_ref.1, f32[1,2048]{1,0:T(1,128)} %bitcast.5, f32[1,2048]{1,0:T(1,128)} %bitcast.6, s32[1,2048]{1,0:T(1,128)} %bitcast.7, ...), custom_call_target="tpu_custom_call" | custom-call | tf_op jit(solution)/shard_map/exchange/pallas_call | solution.py:489
  62.5 4.9 %apply.1 = (f32[144,4096]{1,0:T(8,128)}, f32[144,4096]{1,0:T(8,128)}, f32[1,2048]{1,0:T(1,128)}) custom-call(f32[128,37,128]{2,1,0:T(8,128)} %get-tuple-element.9.received_ref, bf16[288,432]{1,0:T(8,128)(2,1)} %get-tuple-element.10.both_ref, f32[1,2048]{1,0:T(1,128)} %get-tuple-element.11.squares_ref, f32[1,2048]{1,0:T(1,128)} %bitcast.8), custom_call_target="tpu_custom_call" | custom-call | flops 1000000000 | bytes 8000000 | tf_op jit(solution)/shard_map/apply/pallas_call | solution.py:554
